TPU v7x, 512 devices: a whole 4x4x16 slice. The times are simulated.
512 devices in a mesh: tm: 32 (over z, core), col: 16 (over y, x).
Axes of the slice: x: 4, y: 4, z: 16, core: 2. Of those that a mesh axis runs over, the one named last changes fastest.
Arguments:
- diag_blocks: float32 [64, 768, 768], P('tm', 'col'), may hold values from -0.5 to 2, as said below
- left_blocks: float32 [32, 768, 768], P('tm', 'col'), may hold values from -1 to 0.5
- right_blocks: float32 [32, 768, 768], P('tm', 'col'), may hold values from -1 to 0.5
Outputs:
- blocks: float32 [64, 768, 768], P('tm', 'col')
- solved: float32 [32, 2, 768, 768], P('tm', None, 'col')
Inputs may be any that keep to these rules, and one draw needn't show every extreme that they name: `diag_blocks`: every block is symmetric, and together with left_blocks, right_blocks and their transposes it forms a symmetric positive definite matrix.
All inputs are finite; a program needn't handle non-finite values.
Results may differ from a plain program's by a relative error of at most 0.00013.
Values sent between devices are 32-bit elements; how exact they have to be, the bound alone decides.
A program may use at most 64 MiB of HBM per device.

v0:
```python
import jax
import jax.numpy as jnp
from jax import lax
from jax.sharding import PartitionSpec as P


def passed_along(x, axis, by):
    peers = lax.axis_size(axis)
    return lax.ppermute(x, axis, [(i, (i + by) % peers) for i in range(peers)])


def extended(x, sides, width):
    for axis, dim in sides:
        peers, length = (lax.axis_size(axis), x.shape[dim])
        up = [(i, (i + 1) % peers) for i in range(peers)]
        down = [(j, i) for i, j in up]
        last = lax.slice_in_dim(x, length - width, length, axis=dim)
        first = lax.slice_in_dim(x, 0, width, axis=dim)
        before = lax.ppermute(last, axis, up)
        after = lax.ppermute(first, axis, down)
        x = jnp.concatenate([before, x, after], axis=dim)
    return x


def rows_dot(row_part, full_part):
    return lax.dot_general(
        row_part,
        full_part,
        (((1,), (1,)), ((), ())),
        precision=lax.Precision.HIGHEST,
        preferred_element_type=jnp.float32,
    )


def right_solve(factor, target):
    return lax.linalg.triangular_solve(
        factor, target, left_side=False, lower=True, transpose_a=True
    )


def eliminate(pivot_rows, left_rows, right_rows):
    height = pivot_rows.shape[0]
    row_start = lax.axis_index("col") * height
    pivot_full = lax.all_gather(pivot_rows, "col", axis=0, tiled=True)
    factor = jnp.linalg.cholesky(pivot_full)
    solved_left = right_solve(factor, left_rows)
    solved_right = right_solve(factor, right_rows)
    full_left, full_right = (
        lax.all_gather(solved_left, "col", axis=0, tiled=True),
        lax.all_gather(solved_right, "col", axis=0, tiled=True),
    )
    factor_rows = lax.dynamic_slice_in_dim(factor, row_start, height, 0)
    return (
        factor_rows,
        solved_left,
        solved_right,
        full_left,
        full_right,
        solved_left,
        solved_right,
    )


def shards(diag_blocks, left_blocks, right_blocks):
    even_rows = diag_blocks[0]
    odd_rows = diag_blocks[1]
    factor_one, solved_left, solved_right, full_left, full_right, back_left, back_right = eliminate(
        odd_rows, left_blocks[0], right_blocks[0]
    )
    left_gram = rows_dot(back_left, full_left)
    right_gram = rows_dot(back_right, full_right)
    upper_rows = -rows_dot(back_left, full_right)
    mirror_upper = -rows_dot(back_right, full_left)
    right_prev, mirror_lower = passed_along((right_gram, upper_rows), "tm", 1)
    reduced = even_rows - left_gram - right_prev
    factor_two, first_solved, second_solved, first_full, second_full, first_back, second_back = (
        eliminate(reduced, mirror_lower, mirror_upper)
    )
    second_grams = jnp.stack([rows_dot(first_back, first_full), rows_dot(second_back, second_full)])
    halo_rows = extended(second_grams, (("tm", 0),), 1)
    final_block = reduced - halo_rows[3] - halo_rows[0]
    blocks = jnp.stack([final_block, factor_one])
    solved = jnp.stack([solved_left, solved_right])[None]
    return (blocks, solved)


def solution(mesh):
    in_specs = (P("tm", "col", None), P("tm", "col", None), P("tm", "col", None))
    out_specs = (P("tm", "col", None), P("tm", None, "col", None))
    return jax.shard_map(shards, mesh=mesh, in_specs=in_specs, out_specs=out_specs, check_vma=False)
```

profile of v0, /device:TPU:1, one launch (start us, length us, event | category | flops | bytes accessed | tf_op | source)
XLA Modules:
  0.0 874.4 jit_solution(16462688095010835249)
XLA Ops:
  9.0 67.3 %all-gather.18.cloned.1.call-done = f32[1,768,768]{2,0,1:T(1,128)} async-done(((f32[1,48,768]{2,0,1:T(1,128)}), f32[1,768,768]{2,0,1:T(1,128)}) %all-gather.18.cloned.1.call-update) | async-done | bytes 2359312 | tf_op jit(solution)/shard_map/all_gather | solution.py:44
  86.6 11.7 %cholesky.453 = f32[128,128]{1,0:T(8,128)S(1)} custom-call(f32[128,128]{1,0:T(8,128)S(1)} %cholesky.669), custom_call_target="Cholesky" | custom-call | tf_op jit(solution)/shard_map/jit(cholesky)/cholesky | solution.py:45
  98.3 9.8 %custom-call.43 = f32[1,128,128]{1,2,0:T(8,128)S(1)} custom-call(f32[1,128,128]{2,1,0:T(8,128)S(1)} %get-tuple-element.89), custom_call_target="InvertDiagBlocksLowerTriangular" | custom-call | tf_op jit(solution)/shard_map/jit(cholesky)/cholesky | solution.py:45
  111.1 11.7 %cholesky.472 = f32[128,128]{1,0:T(8,128)S(1)} custom-call(f32[128,128]{1,0:T(8,128)S(1)} %cholesky.673), custom_call_target="Cholesky" | custom-call | tf_op jit(solution)/shard_map/jit(cholesky)/cholesky | solution.py:45
  122.8 10.2 %custom-call.44 = f32[1,128,128]{1,2,0:T(8,128)S(1)} custom-call(f32[1,128,128]{2,1,0:T(8,128)S(1)} %get-tuple-element.86), custom_call_target="InvertDiagBlocksLowerTriangular" | custom-call | tf_op jit(solution)/shard_map/jit(cholesky)/cholesky | solution.py:45
  135.0 11.7 %cholesky.493 = f32[128,128]{1,0:T(8,128)S(1)} custom-call(f32[128,128]{1,0:T(8,128)S(1)} %cholesky.678), custom_call_target="Cholesky" | custom-call | tf_op jit(solution)/shard_map/jit(cholesky)/cholesky | solution.py:45
  147.4 9.8 %custom-call.45 = f32[1,128,128]{1,2,0:T(8,128)S(1)} custom-call(f32[1,128,128]{2,1,0:T(8,128)S(1)} %get-tuple-element.83), custom_call_target="InvertDiagBlocksLowerTriangular" | custom-call | tf_op jit(solution)/shard_map/jit(cholesky)/cholesky | solution.py:45
  159.1 11.9 %cholesky.512 = f32[128,128]{1,0:T(8,128)S(1)} custom-call(f32[128,128]{1,0:T(8,128)S(1)} %cholesky.683), custom_call_target="Cholesky" | custom-call | tf_op jit(solution)/shard_map/jit(cholesky)/cholesky | solution.py:45
  171.7 9.8 %custom-call.46 = f32[1,128,128]{1,2,0:T(8,128)S(1)} custom-call(f32[1,128,128]{2,1,0:T(8,128)S(1)} %get-tuple-element.80), custom_call_target="InvertDiagBlocksLowerTriangular" | custom-call | tf_op jit(solution)/shard_map/jit(cholesky)/cholesky | solution.py:45
  183.3 11.7 %cholesky.531 = f32[128,128]{1,0:T(8,128)S(1)} custom-call(f32[128,128]{1,0:T(8,128)S(1)} %cholesky.688), custom_call_target="Cholesky" | custom-call | tf_op jit(solution)/shard_map/jit(cholesky)/cholesky | solution.py:45
  195.7 9.8 %custom-call.47 = f32[1,128,128]{1,2,0:T(8,128)S(1)} custom-call(f32[1,128,128]{2,1,0:T(8,128)S(1)} %get-tuple-element.77), custom_call_target="InvertDiagBlocksLowerTriangular" | custom-call | tf_op jit(solution)/shard_map/jit(cholesky)/cholesky | solution.py:45
  207.1 12.1 %cholesky.548 = f32[128,128]{1,0:T(8,128)S(1)} custom-call(f32[128,128]{1,0:T(8,128)S(1)} %convolution_subtract_fusion.5), custom_call_target="Cholesky" | custom-call | tf_op jit(solution)/shard_map/jit(cholesky)/cholesky | solution.py:45
  226.8 17.4 %while.8 = (s32[]{:T(128)}, f32[768,768]{1,0:T(8,128)}, s32[6,2]{0,1:T(2,128)S(1)}, f32[6,128,128]{2,1,0:T(8,128)S(1)}, s32[]{:T(128)}) while((s32[]{:T(128)}, f32[768,768]{1,0:T(8,128)}, s32[6,2]{0,1:T(2,128)S(1)}, f32[6,128,128]{2,1,0:T(8,128)S(1)}, s32[]{:T(128)}) %tuple.107), condition=%wide.while_cond, body=%wide.while_body.sunk | while | flops 2 | bytes 131189 | solution.py:36
  244.2 59.0 %custom-call.48 = f32[6,128,128]{1,2,0:T(8,128)S(1)} custom-call(f32[6,128,128]{2,1,0:T(8,128)S(1)} %get-tuple-element.30), custom_call_target="InvertDiagBlocksLowerTriangular" | custom-call | tf_op jit(solution)/shard_map/triangular_solve/custom-call.5 | solution.py:36
  319.6 52.2 %all-gather.10.cloned.1.call-done = f32[768,768]{1,0:T(8,128)} async-done(((f32[48,768]{1,0:T(8,128)}), f32[768,768]{1,0:T(8,128)}) %all-gather.10.cloned.1.call-update) | async-done | bytes 2359312 | tf_op jit(solution)/shard_map/all_gather | solution.py:50
  378.9 56.7 %all-gather.8.cloned.1.call-done = f32[768,768]{1,0:T(8,128)} async-done(((f32[48,768]{1,0:T(8,128)}), f32[768,768]{1,0:T(8,128)}) %all-gather.8.cloned.1.call-update) | async-done | bytes 2359312 | tf_op jit(solution)/shard_map/all_gather | solution.py:49
  442.7 58.0 %all-gather.12.cloned.1.call-done = f32[768,768]{1,0:T(8,128)} async-done(((f32[48,768]{1,0:T(8,128)}), f32[768,768]{1,0:T(8,128)}) %all-gather.12.cloned.1.call-update) | async-done | bytes 2359312 | tf_op jit(solution)/shard_map/all_gather | solution.py:44
  507.6 11.7 %cholesky.563 = f32[128,128]{1,0:T(8,128)S(1)} custom-call(f32[128,128]{1,0:T(8,128)S(1)} %cholesky.692), custom_call_target="Cholesky" | custom-call | tf_op jit(solution)/shard_map/jit(cholesky)/cholesky | solution.py:45
  520.0 9.8 %custom-call.50 = f32[1,128,128]{1,2,0:T(8,128)S(1)} custom-call(f32[1,128,128]{2,1,0:T(8,128)S(1)} %get-tuple-element.73), custom_call_target="InvertDiagBlocksLowerTriangular" | custom-call | tf_op jit(solution)/shard_map/jit(cholesky)/cholesky | solution.py:45
  532.8 11.7 %cholesky.582 = f32[128,128]{1,0:T(8,128)S(1)} custom-call(f32[128,128]{1,0:T(8,128)S(1)} %cholesky.696), custom_call_target="Cholesky" | custom-call | tf_op jit(solution)/shard_map/jit(cholesky)/cholesky | solution.py:45
  545.2 10.0 %custom-call.51 = f32[1,128,128]{1,2,0:T(8,128)S(1)} custom-call(f32[1,128,128]{2,1,0:T(8,128)S(1)} %get-tuple-element.70), custom_call_target="InvertDiagBlocksLowerTriangular" | custom-call | tf_op jit(solution)/shard_map/jit(cholesky)/cholesky | solution.py:45
  557.1 11.7 %cholesky.603 = f32[128,128]{1,0:T(8,128)S(1)} custom-call(f32[128,128]{1,0:T(8,128)S(1)} %cholesky.701), custom_call_target="Cholesky" | custom-call | tf_op jit(solution)/shard_map/jit(cholesky)/cholesky | solution.py:45
  569.5 9.8 %custom-call.52 = f32[1,128,128]{1,2,0:T(8,128)S(1)} custom-call(f32[1,128,128]{2,1,0:T(8,128)S(1)} %get-tuple-element.67), custom_call_target="InvertDiagBlocksLowerTriangular" | custom-call | tf_op jit(solution)/shard_map/jit(cholesky)/cholesky | solution.py:45
  581.2 12.1 %cholesky.622 = f32[128,128]{1,0:T(8,128)S(1)} custom-call(f32[128,128]{1,0:T(8,128)S(1)} %cholesky.706), custom_call_target="Cholesky" | custom-call | tf_op jit(solution)/shard_map/jit(cholesky)/cholesky | solution.py:45
  594.1 9.8 %custom-call.53 = f32[1,128,128]{1,2,0:T(8,128)S(1)} custom-call(f32[1,128,128]{2,1,0:T(8,128)S(1)} %get-tuple-element.64), custom_call_target="InvertDiagBlocksLowerTriangular" | custom-call | tf_op jit(solution)/shard_map/jit(cholesky)/cholesky | solution.py:45
  605.7 11.7 %cholesky.641 = f32[128,128]{1,0:T(8,128)S(1)} custom-call(f32[128,128]{1,0:T(8,128)S(1)} %cholesky.711), custom_call_target="Cholesky" | custom-call | tf_op jit(solution)/shard_map/jit(cholesky)/cholesky | solution.py:45
  618.1 9.8 %custom-call.54 = f32[1,128,128]{1,2,0:T(8,128)S(1)} custom-call(f32[1,128,128]{2,1,0:T(8,128)S(1)} %get-tuple-element.61), custom_call_target="InvertDiagBlocksLowerTriangular" | custom-call | tf_op jit(solution)/shard_map/jit(cholesky)/cholesky | solution.py:45
  629.4 11.9 %cholesky.658 = f32[128,128]{1,0:T(8,128)S(1)} custom-call(f32[128,128]{1,0:T(8,128)S(1)} %slice_subtract_fusion.4), custom_call_target="Cholesky" | custom-call | tf_op jit(solution)/shard_map/jit(cholesky)/cholesky | solution.py:45
  647.2 17.3 %while.9 = (s32[]{:T(128)}, f32[768,768]{1,0:T(8,128)}, s32[6,2]{0,1:T(2,128)S(1)}, f32[6,128,128]{2,1,0:T(8,128)S(1)}, s32[]{:T(128)}) while((s32[]{:T(128)}, f32[768,768]{1,0:T(8,128)}, s32[6,2]{0,1:T(2,128)S(1)}, f32[6,128,128]{2,1,0:T(8,128)S(1)}, s32[]{:T(128)}) %tuple.125), condition=%wide.while_cond.clone.1, body=%wide.while_body.clone.1.sunk | while | flops 2 | bytes 131189 | solution.py:36
  665.3 59.8 %custom-call.55 = f32[6,128,128]{1,2,0:T(8,128)S(1)} custom-call(f32[6,128,128]{2,1,0:T(8,128)} %copy-done.15), custom_call_target="InvertDiagBlocksLowerTriangular" | custom-call | tf_op jit(solution)/shard_map/triangular_solve/custom-call.5 | solution.py:36
  749.1 44.3 %all-gather.16.cloned.1.call-done = f32[768,768]{1,0:T(8,128)} async-done(((f32[48,768]{1,0:T(8,128)}), f32[768,768]{1,0:T(8,128)}) %all-gather.16.cloned.1.call-update) | async-done | bytes 2359312 | tf_op jit(solution)/shard_map/all_gather | solution.py:50
  800.7 55.9 %all-gather.14.cloned.1.call-done = f32[768,768]{1,0:T(8,128)} async-done(((f32[48,768]{1,0:T(8,128)}), f32[768,768]{1,0:T(8,128)}) %all-gather.14.cloned.1.call-update) | async-done | bytes 2359312 | tf_op jit(solution)/shard_map/all_gather | solution.py:49
  (215 shorter events, 158.1 us)
Async XLA Ops:
  7.2 69.1 %all-gather.18.cloned.1.call-start = ((), (), s32[]{:S(2)}) async-start(), calls=%async_computation.5 | async-start | bytes 2506752 | tf_op jit(solution)/shard_map/all_gather | solution.py:44
  9.0 362.8 %all-gather.10.cloned.1.call-start = ((), (), s32[]{:S(2)}) async-start(), calls=%async_computation.1 | async-start | bytes 2506752 | tf_op jit(solution)/shard_map/all_gather | solution.py:50
  76.3 6.9 copy-start
  85.1 1.4 copy-start.5
  224.3 78.9 %copy-start.17 = (f32[1,48,768]{2,1,0:T(8,128)S(1)}, f32[1,48,768]{2,1,0:T(8,128)}, u32[]{:S(2)}) copy-start(f32[1,48,768]{2,1,0:T(8,128)} %param.8) | copy-start | bytes 442372
  226.8 84.6 %copy-start.18 = (f32[1,48,768]{2,1,0:T(8,128)S(1)}, f32[1,48,768]{2,1,0:T(8,128)}, u32[]{:S(2)}) copy-start(f32[1,48,768]{2,1,0:T(8,128)} %param.7) | copy-start | bytes 442372
  310.6 0.7 copy-start.8
  311.3 60.4 %copy-start.9 = (f32[48,768]{1,0:T(8,128)S(1)}, f32[48,768]{1,0:T(8,128)}, u32[]{:S(2)}) copy-start(f32[48,768]{1,0:T(8,128)} %copy-done.8) | copy-start | bytes 442372
  311.3 124.2 %all-gather.8.cloned.1.call-start = ((), (), s32[]{:S(2)}) async-start(), calls=%async_computation | async-start | bytes 2506752 | tf_op jit(solution)/shard_map/all_gather | solution.py:49
  314.0 121.6 %copy-start.16 = (f32[2,48,768]{2,1,0:T(8,128)S(1)}, f32[2,48,768]{2,1,0:T(8,128)}, u32[]{:S(2)}) copy-start(f32[2,48,768]{2,1,0:T(8,128)} %param.6) | copy-start | bytes 884740
  318.8 0.7 copy-start.6
  319.5 116.1 %copy-start.7 = (f32[48,768]{1,0:T(8,128)S(1)}, f32[48,768]{1,0:T(8,128)}, u32[]{:S(2)}) copy-start(f32[48,768]{1,0:T(8,128)} %copy-done.6) | copy-start | bytes 442372
  319.5 181.2 %all-gather.12.cloned.1.call-start = ((), (), s32[]{:S(2)}) async-start(), calls=%async_computation.2 | async-start | bytes 2506752 | tf_op jit(solution)/shard_map/all_gather | solution.py:44
  375.7 59.9 %collective-permute-start = (f32[48,768]{1,0:T(8,128)S(1)}, f32[48,768]{1,0:T(8,128)S(1)}, u32[]{:S(2)}, u32[]{:S(2)}) collective-permute-start(f32[48,768]{1,0:T(8,128)S(1)} %fusion.179), channel_id=1, source_target_pairs={{0,16},{16,32},{32,48},{48,64},{64,80},{80,96},{96,112},{112,128},... | collective-permute-start | bytes 442376 | tf_op jit(solution)/shard_map/ppermute | solution.py:9
  435.6 4.8 copy-start.3
  440.4 353.1 %all-gather.16.cloned.1.call-start = ((), (), s32[]{:S(2)}) async-start(), calls=%async_computation.4 | async-start | bytes 2506752 | tf_op jit(solution)/shard_map/all_gather | solution.py:50
  500.7 3.4 copy-start.1
  506.1 1.4 copy-start.4
  647.2 86.2 %copy-start.2 = (f32[768,768]{1,0:T(8,128)S(1)}, f32[768,768]{1,0:T(8,128)}, u32[]{:S(2)}) copy-start(f32[768,768]{1,0:T(8,128)} %all-gather.10.cloned.1.call-done) | copy-start | bytes 7077892
  664.5 0.7 copy-start.15
  732.4 0.7 copy-start.11
  733.1 60.4 %copy-start.12 = (f32[48,768]{1,0:T(8,128)S(1)}, f32[48,768]{1,0:T(8,128)}, u32[]{:S(2)}) copy-start(f32[48,768]{1,0:T(8,128)} %copy-done.11) | copy-start | bytes 442372
  733.1 123.5 %all-gather.14.cloned.1.call-start = ((), (), s32[]{:S(2)}) async-start(), calls=%async_computation.3 | async-start | bytes 2506752 | tf_op jit(solution)/shard_map/all_gather | solution.py:49
  735.7 5.3 collective-permute-start.1
  748.5 0.7 copy-start.13
  749.1 107.5 %copy-start.14 = (f32[48,768]{1,0:T(8,128)S(1)}, f32[48,768]{1,0:T(8,128)}, u32[]{:S(2)}) copy-start(f32[48,768]{1,0:T(8,128)} %copy-done.13) | copy-start | bytes 442372
  797.4 69.2 %copy-start.10 = (f32[48,768]{1,0:T(8,128)S(1)}, f32[48,768]{1,0:T(8,128)}, u32[]{:S(2)}) copy-start(f32[48,768]{1,0:T(8,128)} %fusion.4) | copy-start | bytes 442372
  797.5 66.8 %collective-permute-start.3 = (f32[1,48,768]{2,1,0:T(8,128)S(1)}, f32[1,48,768]{2,1,0:T(8,128)S(1)}, u32[]{:S(2)}, u32[]{:S(2)}) collective-permute-start(f32[1,48,768]{2,1,0:T(8,128)S(1)} %convolution_bitcast_fusion), channel_id=1, source_target_pairs={{0,16},{16,32},{32,48},{48,64},{64,80},{80,96},{96,112},{112,128},... | collective-permute-start | bytes 442376 | tf_op jit(solution)/shard_map/ppermute | solution.py:19
  860.5 6.1 collective-permute-start.2
Sparse Core Ops, SparseCore 0:
  11.6 64.6 all-gather.17
  311.4 60.2 all-gather.9
  375.3 60.1 all-gather.7
  440.5 60.1 all-gather.11
  733.3 60.1 all-gather.15
  796.4 60.1 all-gather.13
where the time goes:
time: 885 us; the launch traced here: 874 us
  other arithmetic  376 us (42%)
  waiting for transfers between devices  339 us (38%)
  matrix products  70.1 us (8%)
  local copies, waits for them, and re-layouts  54 us (6%)
  between operations  22.7 us (3%)
  starting transfers between devices  12.2 us (1%)
    another operation x45, other arithmetic, eliminate(): factor = jnp.linalg.cholesky(pivot_full)  248 us
    all_gather x2, waiting for transfers between devices, eliminate(): pivot_full = lax.all_gather(pivot_rows, 'col', axis=0, tiled=True)  125 us
    another operation x5, other arithmetic, right_solve(): lax.linalg.triangular_solve(factor, target, left_side=False, lower=True,...  123 us
    all_gather x2, waiting for transfers between devices, eliminate(): lax.all_gather(solved_left, 'col', axis=0, tiled=True)  113 us
    all_gather x2, waiting for transfers between devices, eliminate(): lax.all_gather(solved_right, 'col', axis=0, tiled=True)  96.5 us
    another operation x39, local copies, waits for them, and re-layouts, right_solve(): lax.linalg.triangular_solve(factor, target, left_side=False, lower=True,...  34.5 us
    another operation x44, matrix products, right_solve(): lax.linalg.triangular_solve(factor, target, left_side=False, lower=True,...  29.3 us
    dot_general x6, matrix products, rows_dot(): lax.dot_general(row_part, full_part, (((1,), (1,)), ((), ())), precision=...  21.1 us
  transfers between devices with their start and end apart: 10, of which 8 were waited for; matrix products, arithmetic and copies ran while one was open for 4% of the time, Pallas kernels for 0%

commit v1 on v0

v1 whole, which is shorter than its diff:
```python
import functools
import jax
import jax.numpy as jnp
from jax import lax
from jax.experimental import pallas as pl
from jax.experimental.pallas import tpu as pltpu
from jax.sharding import PartitionSpec as P

F32 = jnp.float32
BF16 = jnp.bfloat16
NT = 128
NN = (((1,), (0,)), ((), ()))
NTR = (((1,), (1,)), ((), ()))
TN = (((0,), (0,)), ((), ()))


def split(x):
    hi = x.astype(BF16)
    lo = (x - hi.astype(F32)).astype(BF16)
    return hi, lo


def bdot(a, b, dims):
    return lax.dot_general(a, b, dims, preferred_element_type=F32)


def dot3(a, b, dims):
    ah, al = a
    bh, bl = b
    return bdot(ah, bh, dims) + (bdot(ah, bl, dims) + bdot(al, bh, dims))


def lane(row, j):
    return jnp.broadcast_to(row[:, j:j + 1], (1, NT))


def factor_diag(d_ref, e_ref):
    row = lax.broadcasted_iota(jnp.int32, (NT, NT), 0)
    col = lax.broadcasted_iota(jnp.int32, (NT, NT), 1)
    e_ref[...] = jnp.where(row == col, 1.0, 0.0).astype(F32)
    us, es = None, None
    strips = NT // 8
    for s in range(strips):
        b = 8 * s
        d = [d_ref[b + i:b + i + 1, :] for i in range(8)]
        e = [e_ref[b + i:b + i + 1, :] for i in range(8)]
        p = {(i, j): lane(d[i], b + j) for i in range(8) for j in range(i + 1)}
        if us is not None:
            q = [[lane(us[k], b + i) for i in range(8)] for k in range(8)]
            for i in range(8):
                for j in range(i + 1):
                    acc = q[0][i] * q[0][j]
                    for k in range(1, 8):
                        acc = acc + q[k][i] * q[k][j]
                    p[i, j] = p[i, j] - acc
                acc_d = q[0][i] * us[0]
                acc_e = q[0][i] * es[0]
                for k in range(1, 8):
                    acc_d = acc_d + q[k][i] * us[k]
                    acc_e = acc_e + q[k][i] * es[k]
                d[i] = d[i] - acc_d
                e[i] = e[i] - acc_e
        for k in range(8):
            r = lax.rsqrt(p[k, k])
            d[k] = d[k] * r
            e[k] = e[k] * r
            for i in range(k + 1, 8):
                p[i, k] = p[i, k] * r
            for i in range(k + 1, 8):
                for j in range(k + 1, i + 1):
                    p[i, j] = p[i, j] - p[i, k] * p[j, k]
                d[i] = d[i] - p[i, k] * d[k]
                e[i] = e[i] - p[i, k] * e[k]
        us, es = d, e
        for i in range(8):
            d_ref[b + i:b + i + 1, :] = d[i]
            e_ref[b + i:b + i + 1, :] = e[i]
        if s + 2 < strips:
            lo_row = b + 16
            u8 = d_ref[b:b + 8, :]
            e8 = e_ref[b:b + 8, :]
            w = jnp.concatenate([u8, e8], axis=1)
            wh = w.astype(BF16).astype(F32)
            wl = w - wh
            rhs = jnp.concatenate([wh, wl, wh, wl], axis=0).astype(BF16)
            uh, ul = wh[:, :NT], wl[:, :NT]
            lhs = jnp.concatenate([uh, uh, ul, ul], axis=0).astype(BF16)
            upd = bdot(lhs, rhs, TN)[lo_row:, :]
            d_ref[lo_row:, :] = d_ref[lo_row:, :] - upd[:, :NT]
            e_ref[lo_row:, :] = e_ref[lo_row:, :] - upd[:, NT:]


MESH = pl.DeviceIdType.MESH


def reduce_block(blocks, a_ref, z_ref, linv_ref, d_ref, e_ref, keep_factor):
    size = blocks * NT
    rows = a_ref.shape[0]

    def step(j, carry):
        at = pl.ds(pl.multiple_of(j * NT, NT), NT)
        d_ref[...] = a_ref[at, at]
        factor_diag(d_ref, e_ref)
        linv_ref[j] = e_ref[...]
        if keep_factor:
            a_ref[at, at] = d_ref[...].T
        for i in range(blocks):

            @pl.when(j == i)
            def _():
                cols = slice(i * NT, (i + 1) * NT)
                below = (i + 1) * NT
                panel = dot3(split(a_ref[below:, cols]), split(e_ref[...]), NTR)
                a_ref[below:, cols] = panel
                ph, pw = split(panel)
                for k in range(i + 1, blocks):
                    r = k * NT
                    o = r - below
                    new = dot3((ph[o:], pw[o:]), (ph[o:o + NT], pw[o:o + NT]), NTR)
                    a_ref[r:, r:r + NT] = a_ref[r:, r:r + NT] - new

        return carry

    lax.fori_loop(0, blocks, step, 0)
    for i in reversed(range(blocks)):
        cols = slice(i * NT, (i + 1) * NT)
        below = (i + 1) * NT
        acc = a_ref[size:rows, cols]
        if below < size:
            acc = acc - dot3(split(z_ref[:, below:]), split(a_ref[below:size, cols]), NN)
        z_ref[:, cols] = dot3(split(acc), split(linv_ref[i]), NN)


def level_one(pivot, left, right, factor, solved, lgram, rgram, upper, mirror, a_ref, z_ref, linv_ref, d_ref, e_ref):
    size = pivot.shape[0]
    height = factor.shape[0]
    start = pl.multiple_of(lax.axis_index("col") * height, 16)
    mine = pl.ds(start, height)
    a_ref[:size, :] = pivot[...]
    a_ref[size:size + height, :] = left[mine, :]
    a_ref[size + height:, :] = right[mine, :]
    reduce_block(size // NT, a_ref, z_ref, linv_ref, d_ref, e_ref, True)
    row = start + lax.broadcasted_iota(jnp.int32, (height, size), 0)
    col = lax.broadcasted_iota(jnp.int32, (height, size), 1)
    factor[...] = jnp.where(col <= row, a_ref[mine, :], 0.0)
    solved[0] = a_ref[size:size + height, :]
    solved[1] = a_ref[size + height:, :]
    z = split(z_ref[...])
    for n in range(0, size, 256):
        cols = slice(n, n + 256)
        with_left = dot3(z, split(left[cols, :]), NTR)
        with_right = dot3(z, split(right[cols, :]), NTR)
        lgram[:, cols] = with_left[:height]
        mirror[:, cols] = -with_left[height:]
        upper[:, cols] = -with_right[:height]
        rgram[:, cols] = with_right[height:]


def level_two(pivot, first, second, fgram, sgram, a_ref, z_ref, linv_ref, d_ref, e_ref):
    size = pivot.shape[0]
    height = fgram.shape[0]
    mine = pl.ds(pl.multiple_of(lax.axis_index("col") * height, 16), height)
    a_ref[:size, :] = pivot[...]
    a_ref[size:size + height, :] = first[mine, :]
    a_ref[size + height:, :] = second[mine, :]
    reduce_block(size // NT, a_ref, z_ref, linv_ref, d_ref, e_ref, False)
    zf = split(z_ref[:height, :])
    zs = split(z_ref[height:, :])
    for n in range(0, size, 256):
        cols = slice(n, n + 256)
        fgram[:, cols] = dot3(zf, split(first[cols, :]), NTR)
        sgram[:, cols] = dot3(zs, split(second[cols, :]), NTR)


def ring(axis, by):
    return lax.rem(lax.axis_index(axis) + by, lax.axis_size(axis))


def enter(peers):
    barrier = pltpu.get_barrier_semaphore()
    for peer in peers:
        pl.semaphore_signal(barrier, inc=1, device_id=peer, device_id_type=MESH)
    pl.semaphore_wait(barrier, len(peers))


def to_all(src, full, send, recv, n, height):
    mine = pl.ds(lax.axis_index("col") * height, height)
    copies = []
    for by in range(1, n):
        copies.append(
            pltpu.make_async_remote_copy(
                src_ref=src,
                dst_ref=full.at[mine],
                send_sem=send.at[by],
                recv_sem=recv.at[by],
                device_id={"col": ring("col", by)},
                device_id_type=MESH,
            )
        )
    for copy in copies:
        copy.start()
    return copies


def gather_kernel(n, odd, left, right, odd_full, left_full, right_full, send, recv):
    height = odd.shape[0]
    enter([{"col": ring("col", by)} for by in range(1, n)])
    mine = pl.ds(pl.multiple_of(lax.axis_index("col") * height, 16), height)
    copies = []
    for i, (src, full) in enumerate(((odd, odd_full), (left, left_full), (right, right_full))):
        copies += to_all(src, full, send.at[i], recv.at[i], n, height)
    for src, full in ((odd, odd_full), (left, left_full), (right, right_full)):
        full[mine, :] = src[...]
    for copy in copies:
        copy.wait()


def next_kernel(n, t, even, lgram, rgram, upper, mirror, reduced, pivot, first, second, came, send, recv, tsend, trecv):
    height = even.shape[0]
    enter(
        [{"col": ring("col", by)} for by in range(1, n)]
        + [{"tm": ring("tm", 1)}, {"tm": ring("tm", t - 1)}]
    )
    mine = pl.ds(pl.multiple_of(lax.axis_index("col") * height, 16), height)

    def onward(i, src, dst):
        return pltpu.make_async_remote_copy(
            src_ref=src,
            dst_ref=dst,
            send_sem=tsend.at[i],
            recv_sem=trecv.at[i],
            device_id={"tm": ring("tm", 1)},
            device_id_type=MESH,
        )

    over_gram = onward(0, rgram, came)
    over_upper = onward(1, upper, first.at[mine])
    over_gram.start()
    over_upper.start()
    kept = even[...] - lgram[...]
    second[mine, :] = mirror[...]
    over_gram.wait_recv()
    kept = kept - came[...]
    reduced[...] = kept
    pivot[mine, :] = kept
    copies = to_all(reduced, pivot, send.at[0], recv.at[0], n, height)
    over_upper.wait_recv()
    copies += to_all(first.at[mine], first, send.at[1], recv.at[1], n, height)
    copies += to_all(mirror, second, send.at[2], recv.at[2], n, height)
    over_gram.wait_send()
    over_upper.wait_send()
    for copy in copies:
        copy.wait()


def last_kernel(t, reduced, fgram, sgram, final, came, send, recv):
    enter([{"tm": ring("tm", 1)}, {"tm": ring("tm", t - 1)}])
    copies = []
    for i, (src, by) in enumerate(((fgram, t - 1), (sgram, 1))):
        copies.append(
            pltpu.make_async_remote_copy(
                src_ref=src,
                dst_ref=came.at[i],
                send_sem=send.at[i],
                recv_sem=recv.at[i],
                device_id={"tm": ring("tm", by)},
                device_id_type=MESH,
            )
        )
    for copy in copies:
        copy.start()
    for copy in copies:
        copy.wait()
    final[...] = reduced[...] - came[0] - came[1]


def call(kernel, outs, scratch, remote, *args):
    side = {"collective_id": remote, "has_side_effects": True} if remote is not None else {}
    return pl.pallas_call(
        kernel,
        out_shape=[jax.ShapeDtypeStruct(s, F32) for s in outs],
        in_specs=[pl.BlockSpec(memory_space=pltpu.VMEM)] * len(args),
        out_specs=[pl.BlockSpec(memory_space=pltpu.VMEM)] * len(outs),
        scratch_shapes=scratch,
        compiler_params=pltpu.CompilerParams(vmem_limit_bytes=56 << 20, **side),
    )(*args)


def solution(mesh):
    n, t = mesh.shape["col"], mesh.shape["tm"]

    def shards(diag_blocks, left_blocks, right_blocks):
        even, odd = diag_blocks[0], diag_blocks[1]
        height, size = odd.shape
        part, full = (height, size), (size, size)
        sems = [pltpu.SemaphoreType.DMA((3, n))] * 2
        work = [
            pltpu.VMEM((size + 2 * height, size), F32),
            pltpu.VMEM((2 * height, size), F32),
            pltpu.VMEM((size // NT, NT, NT), F32),
            pltpu.VMEM((NT, NT), F32),
            pltpu.VMEM((NT, NT), F32),
        ]
        pivot, left, right = call(
            functools.partial(gather_kernel, n), [full] * 3, sems, 0, odd, left_blocks[0], right_blocks[0]
        )
        factor, solved, lgram, rgram, upper, mirror = call(
            level_one, [part, (2, *part)] + [part] * 4, work, None, pivot, left, right
        )
        two = [pltpu.SemaphoreType.DMA((2,))] * 2
        reduced, pivot, first, second = call(
            functools.partial(next_kernel, n, t),
            [part, full, full, full],
            [pltpu.VMEM(part, F32)] + sems + two,
            1,
            even,
            lgram,
            rgram,
            upper,
            mirror,
        )
        fgram, sgram = call(level_two, [part] * 2, work, None, pivot, first, second)
        (final,) = call(
            functools.partial(last_kernel, t), [part], [pltpu.VMEM((2, *part), F32)] + two, 2, reduced, fgram, sgram
        )
        return jnp.stack([final, factor]), solved[None]

    in_specs = (P("tm", "col", None), P("tm", "col", None), P("tm", "col", None))
    out_specs = (P("tm", "col", None), P("tm", None, "col", None))
    return jax.shard_map(shards, mesh=mesh, in_specs=in_specs, out_specs=out_specs, check_vma=False)
```

time: 885 us -> 304 us (0.34); the launches traced: 874 us -> 304 us
  other arithmetic: 376 us -> 1.64 us
  waiting for transfers between devices: 339 us -> 0 us
  Pallas kernels: 0 us -> 299 us
  matrix products: 70.1 us -> 0 us
  local copies, waits for them, and re-layouts: 54 us -> 1.71 us
  between operations: 22.7 us -> 0.67 us
  starting transfers between devices: 12.2 us -> 0 us
    another operation x52 -> x1, other arithmetic: 372 us -> 1.64 us  [shards(): return (jnp.stack([final, factor]), solved[None])]
    all_gather x6 -> x0, waiting for transfers between devices: 334 us -> none  [the longest x2 125 us: eliminate(): pivot_full = lax.all_gather(pivot_rows, 'col', axis=0, tiled=True)]
    pallas_call x0 -> x5, Pallas kernels: none -> 299 us  [call(): pl.pallas_call(kernel, out_shape=[jax.ShapeDtypeStruct(s, F32) for s in o...]
    another operation x64 -> x0, matrix products: 49 us -> none  [the longest x44 29.3 us: right_solve(): lax.linalg.triangular_solve(factor, target, left_side=False, lower=True,...]
    another operation x52 -> x0, local copies, waits for them, and re-layouts: 35.8 us -> none  [the longest x39 34.5 us: right_solve(): lax.linalg.triangular_solve(factor, target, left_side=False, lower=True,...]
    dot_general x6 -> x0, matrix products: 21.1 us -> none  [rows_dot(): lax.dot_general(row_part, full_part, (((1,), (1,)), ((), ())), precision=...]
    ppermute x4 -> x0, starting transfers between devices: 11.8 us -> none  [the longest x2 6.46 us: passed_along(): return lax.ppermute(x, axis, [(i, (i + by) % peers) for i in range(peers)])]
    all_gather x2 -> x0, local copies, waits for them, and re-layouts: 10.3 us -> none  [eliminate(): pivot_full = lax.all_gather(pivot_rows, 'col', axis=0, tiled=True)]
  transfers between devices with their start and end apart: 10 -> 0, of which waited for: 8 -> 0; matrix products, arithmetic and copies ran while one was open for 4% -> 0% of each run, Pallas kernels for 0% -> 0%
where the time goes in v1:
time: 304 us
  Pallas kernels  299 us (98%)
    pallas_call x5, Pallas kernels, call(): pl.pallas_call(kernel, out_shape=[jax.ShapeDtypeStruct(s, F32) for s in o...  299 us

profile of v1, /device:TPU:1, one launch (start us, length us, event | category | flops | bytes accessed | tf_op | source)
XLA Modules:
  0.0 303.5 jit_solution(16433805268256864981)
XLA Ops:
  0.6 1.7 slice_bitcast_fusion.1
  2.3 98.1 %shard_map.50 = (f32[768,768]{1,0:T(8,128)}, f32[768,768]{1,0:T(8,128)}, f32[768,768]{1,0:T(8,128)}) custom-call(f32[48,768]{1,0:T(8,128)} %get-tuple-element.33.odd, f32[48,768]{1,0:T(8,128)} %bitcast.10, f32[48,768]{1,0:T(8,128)} %bitcast.11), custom_call_target="tpu_custom_call" | custom-call | tf_op jit(solution)/shard_map/pallas_call | solution.py:279
  100.4 41.6 %shard_map.51 = (f32[48,768]{1,0:T(8,128)}, f32[2,48,768]{2,1,0:T(8,128)}, f32[48,768]{1,0:T(8,128)}, f32[48,768]{1,0:T(8,128)}, f32[48,768]{1,0:T(8,128)}, /*index=5*/f32[48,768]{1,0:T(8,128)}) custom-call(f32[768,768]{1,0:T(8,128)} %get-tuple-element.17.pivot, f32[768,768]{1,0:T(8,128)} %get-tuple-element.18.left, f32[768,768]{1,0:T(8,128)} %get-tuple-element.19.right), custom_call_target="tpu_custom_call" | custom-call | tf_op jit(solution)/shard_map/pallas_call | solution.py:279
  142.1 97.5 %shard_map.52 = (f32[48,768]{1,0:T(8,128)}, f32[768,768]{1,0:T(8,128)}, f32[768,768]{1,0:T(8,128)}, f32[768,768]{1,0:T(8,128)}) custom-call(f32[48,768]{1,0:T(8,128)} %get-tuple-element.32.even, f32[48,768]{1,0:T(8,128)} %get-tuple-element.20.lgram, f32[48,768]{1,0:T(8,128)} %get-tuple-element.21.rgram, f32[48,768]{1,0:T(8,128)} %get-tuple-element.22.upper, ...), custom_call_target="tpu_custom_call" | custom-call | tf_op jit(solution)/shard_map/pallas_call | solution.py:279
  239.5 0.0 copy-start
  239.5 41.3 %shard_map.53 = (f32[48,768]{1,0:T(8,128)}, f32[48,768]{1,0:T(8,128)}) custom-call(f32[768,768]{1,0:T(8,128)} %get-tuple-element.25.pivot, f32[768,768]{1,0:T(8,128)} %get-tuple-element.26.first, f32[768,768]{1,0:T(8,128)} %get-tuple-element.27.second), custom_call_target="tpu_custom_call" | custom-call | tf_op jit(solution)/shard_map/pallas_call | solution.py:279
  280.8 21.0 %shard_map.54 = f32[48,768]{1,0:T(8,128)} custom-call(f32[48,768]{1,0:T(8,128)} %get-tuple-element.24.reduced, f32[48,768]{1,0:T(8,128)} %get-tuple-element.28.fgram, f32[48,768]{1,0:T(8,128)} %get-tuple-element.29.sgram), custom_call_target="tpu_custom_call" | custom-call | tf_op jit(solution)/shard_map/pallas_call | solution.py:279
  301.9 0.0 copy-done
  301.9 1.6 pad_maximum_fusion
Async XLA Ops:
  239.5 62.3 %copy-start = (f32[48,768]{1,0:T(8,128)S(1)}, f32[48,768]{1,0:T(8,128)}, u32[]{:S(2)}) copy-start(f32[48,768]{1,0:T(8,128)} %get-tuple-element.30) | copy-start | bytes 442372

commit v2 on v1

v2 whole, which is shorter than its diff:
```python
import jax
import jax.numpy as jnp
from jax import lax
from jax.experimental import pallas as pl
from jax.experimental.pallas import tpu as pltpu
from jax.sharding import PartitionSpec as P

F32 = jnp.float32
BF16 = jnp.bfloat16
NT = 128
NN = (((1,), (0,)), ((), ()))
NTR = (((1,), (1,)), ((), ()))
TN = (((0,), (0,)), ((), ()))


def split(x):
    hi = x.astype(BF16)
    lo = (x - hi.astype(F32)).astype(BF16)
    return hi, lo


def bdot(a, b, dims):
    return lax.dot_general(a, b, dims, preferred_element_type=F32)


def dot3(a, b, dims):
    ah, al = a
    bh, bl = b
    return bdot(ah, bh, dims) + (bdot(ah, bl, dims) + bdot(al, bh, dims))


def lane(row, j):
    return jnp.broadcast_to(row[:, j:j + 1], (1, NT))


def factor_diag(d_ref, e_ref):
    row = lax.broadcasted_iota(jnp.int32, (NT, NT), 0)
    col = lax.broadcasted_iota(jnp.int32, (NT, NT), 1)
    e_ref[...] = jnp.where(row == col, 1.0, 0.0).astype(F32)
    us, es = None, None
    strips = NT // 8
    for s in range(strips):
        b = 8 * s
        d = [d_ref[b + i:b + i + 1, :] for i in range(8)]
        e = [e_ref[b + i:b + i + 1, :] for i in range(8)]
        p = {(i, j): lane(d[i], b + j) for i in range(8) for j in range(i + 1)}
        if us is not None:
            q = [[lane(us[k], b + i) for i in range(8)] for k in range(8)]
            for i in range(8):
                for j in range(i + 1):
                    acc = q[0][i] * q[0][j]
                    for k in range(1, 8):
                        acc = acc + q[k][i] * q[k][j]
                    p[i, j] = p[i, j] - acc
                acc_d = q[0][i] * us[0]
                acc_e = q[0][i] * es[0]
                for k in range(1, 8):
                    acc_d = acc_d + q[k][i] * us[k]
                    acc_e = acc_e + q[k][i] * es[k]
                d[i] = d[i] - acc_d
                e[i] = e[i] - acc_e
        for k in range(8):
            r = lax.rsqrt(p[k, k])
            d[k] = d[k] * r
            e[k] = e[k] * r
            for i in range(k + 1, 8):
                p[i, k] = p[i, k] * r
            for i in range(k + 1, 8):
                for j in range(k + 1, i + 1):
                    p[i, j] = p[i, j] - p[i, k] * p[j, k]
                d[i] = d[i] - p[i, k] * d[k]
                e[i] = e[i] - p[i, k] * e[k]
        us, es = d, e
        for i in range(8):
            d_ref[b + i:b + i + 1, :] = d[i]
            e_ref[b + i:b + i + 1, :] = e[i]
        if s + 2 < strips:
            lo_row = b + 16
            u8 = d_ref[b:b + 8, :]
            e8 = e_ref[b:b + 8, :]
            w = jnp.concatenate([u8, e8], axis=1)
            wh = w.astype(BF16).astype(F32)
            wl = w - wh
            rhs = jnp.concatenate([wh, wl, wh, wl], axis=0).astype(BF16)
            uh, ul = wh[:, :NT], wl[:, :NT]
            lhs = jnp.concatenate([uh, uh, ul, ul], axis=0).astype(BF16)
            upd = bdot(lhs, rhs, TN)[lo_row:, :]
            d_ref[lo_row:, :] = d_ref[lo_row:, :] - upd[:, :NT]
            e_ref[lo_row:, :] = e_ref[lo_row:, :] - upd[:, NT:]


MESH = pl.DeviceIdType.MESH


def reduce_block(blocks, a_ref, z_ref, linv_ref, d_ref, e_ref, keep_factor, during):
    size = blocks * NT
    rows = a_ref.shape[0]

    def step(j, carry):
        at = pl.ds(pl.multiple_of(j * NT, NT), NT)
        d_ref[...] = a_ref[at, at]
        factor_diag(d_ref, e_ref)
        linv_ref[j] = e_ref[...]
        if keep_factor:
            a_ref[at, at] = d_ref[...].T
        for i in range(blocks):

            @pl.when(j == i)
            def _():
                during(i)
                cols = slice(i * NT, (i + 1) * NT)
                below = (i + 1) * NT
                panel = dot3(split(a_ref[below:, cols]), split(e_ref[...]), NTR)
                a_ref[below:, cols] = panel
                ph, pw = split(panel)
                for k in range(i + 1, blocks):
                    r = k * NT
                    o = r - below
                    new = dot3((ph[o:], pw[o:]), (ph[o:o + NT], pw[o:o + NT]), NTR)
                    a_ref[r:, r:r + NT] = a_ref[r:, r:r + NT] - new

        return carry

    lax.fori_loop(0, blocks, step, 0)
    for i in reversed(range(blocks)):
        cols = slice(i * NT, (i + 1) * NT)
        below = (i + 1) * NT
        acc = a_ref[size:rows, cols]
        if below < size:
            acc = acc - dot3(split(z_ref[:, below:]), split(a_ref[below:size, cols]), NN)
        z_ref[:, cols] = dot3(split(acc), split(linv_ref[i]), NN)


def wrap(axis, by):
    size = lax.axis_size(axis)
    return lax.rem(lax.axis_index(axis) + (by + size), size)


def plus(a, b):
    return (a[0] + b[0], a[1] + b[1])


def times(k, a):
    return (k * a[0], k * a[1])


def torus_plan():
    whole, top, bottom = (0, 2), (0, 1), (1, 2)
    messages, rounds = [], []

    def leave(towards, block, rows, part):
        messages.append((towards, block, rows, part))
        return len(messages) - 1

    def relay(axis, block, part):
        return [
            leave(axis, plus(block, times(-1, axis)), top, part),
            leave(times(-1, axis), plus(block, axis), bottom, part),
        ]

    def both(axis, block, part):
        return [leave(axis, block, whole, part), leave(times(-1, axis), block, whole, part)]

    rings = ((0, 1), (1, 0))
    own = [m for axis in rings for m in both(axis, (0, 0), None)]
    rounds.append(([], own))
    far, sides, starts = [], [], []
    for part in range(2):
        a, b = rings[part], rings[1 - part]
        far.append(relay(a, (0, 0), part))
        sides.append([both(b, times(-1, a), part), both(b, a, part)])
        starts += far[part] + sides[part][0] + sides[part][1] + relay(b, (0, 0), part)
    rounds.append((own, starts))
    comes, starts, last = [], [], []
    for part in range(2):
        a, b = rings[part], rings[1 - part]
        comes += far[part] + sides[part][0] + sides[part][1]
        last.append(both(b, times(2, a), part))
        starts += last[part] + relay(b, times(-1, a), part) + relay(b, a, part)
    rounds.append((comes, starts))
    starts = []
    for part in range(2):
        a, b = rings[part], rings[1 - part]
        starts += relay(b, times(2, a), part)
    rounds.append((last[0] + last[1], starts))
    seen = {m for came, _ in rounds for m in came}
    rounds.append(([m for m in range(len(messages)) if m not in seen], []))
    return messages, rounds


MESSAGES, ROUNDS = torus_plan()
SIDE = 4


def gather_round(k, arrays):
    me = lax.axis_index("col")
    y, x = lax.div(me, SIDE), lax.rem(me, SIDE)

    def device(by):
        return lax.rem(y + (by[0] + SIDE), SIDE) * SIDE + lax.rem(x + (by[1] + SIDE), SIDE)

    def message(i, src, full, send, recv):
        towards, block, rows, part = MESSAGES[i]
        height, width = full.shape[0] // SIDE**2, full.shape[1]
        begin, length = rows[0] * height // 2, (rows[1] - rows[0]) * height // 2
        at = pl.ds(pl.multiple_of(device(block) * height + begin, 8), length)
        cols = pl.ds(0, width) if part is None else pl.ds(part * (width // 2), width // 2)
        there = full.at[at, cols]
        here = src if block == (0, 0) and part is None else there
        return pltpu.make_async_remote_copy(
            src_ref=here,
            dst_ref=there,
            send_sem=send.at[i],
            recv_sem=recv.at[i],
            device_id={"col": device(towards)},
            device_id_type=MESH,
        )

    comes, starts = ROUNDS[k]
    for array in arrays:
        for i in comes:
            message(i, *array).wait_recv()
    for array in arrays:
        for i in starts:
            message(i, *array).start()
    if k == len(ROUNDS) - 1:
        for array in arrays:
            for i in range(len(MESSAGES)):
                message(i, *array).wait_send()


def enter(others):
    me = lax.axis_index("col")
    y, x = lax.div(me, SIDE), lax.rem(me, SIDE)
    peers = [
        {"col": lax.rem(y + (dy + SIDE), SIDE) * SIDE + lax.rem(x + (dx + SIDE), SIDE)}
        for dy, dx in ((0, 1), (0, -1), (1, 0), (-1, 0))
    ] + others
    barrier = pltpu.get_barrier_semaphore()
    for peer in peers:
        pl.semaphore_signal(barrier, inc=1, device_id=peer, device_id_type=MESH)
    pl.semaphore_wait(barrier, len(peers))


def my_rows(height):
    return pl.ds(pl.multiple_of(lax.axis_index("col") * height, 16), height)


def level_one(diag, left, right, factor, solved, lgram, rgram, upper, mirror, *scratch):
    a_ref, z_ref, linv_ref, d_ref, e_ref, left_full, right_full, send, recv = scratch
    size = left_full.shape[0]
    height = factor.shape[0]
    mine = my_rows(height)
    enter([])
    pivot = [(diag.at[1], a_ref.at[pl.ds(0, size)], send.at[0], recv.at[0])]
    couplings = [
        (left, left_full, send.at[1], recv.at[1]),
        (right, right_full, send.at[2], recv.at[2]),
    ]
    gather_round(0, pivot)
    a_ref[mine, :] = diag[1]
    a_ref[size:size + height, :] = left[...]
    a_ref[size + height:, :] = right[...]
    left_full[mine, :] = left[...]
    right_full[mine, :] = right[...]
    for k in range(1, 4):
        gather_round(k, pivot)
    gather_round(0, couplings)
    gather_round(4, pivot)

    def during(j):
        if j < 3:
            gather_round(j + 1, couplings)

    reduce_block(size // NT, a_ref, z_ref, linv_ref, d_ref, e_ref, True, during)
    row = lax.axis_index("col") * height + lax.broadcasted_iota(jnp.int32, (height, size), 0)
    col = lax.broadcasted_iota(jnp.int32, (height, size), 1)
    factor[...] = jnp.where(col <= row, a_ref[mine, :], 0.0)
    solved[0] = a_ref[size:size + height, :]
    solved[1] = a_ref[size + height:, :]
    gather_round(4, couplings)
    z = split(z_ref[...])
    for n in range(0, size, 256):
        cols = slice(n, n + 256)
        with_left = dot3(z, split(left_full[cols, :]), NTR)
        with_right = dot3(z, split(right_full[cols, :]), NTR)
        lgram[:, cols] = with_left[:height]
        mirror[:, cols] = -with_left[height:]
        upper[:, cols] = -with_right[:height]
        rgram[:, cols] = with_right[height:]


def level_two(diag, factor, lgram, rgram, upper, mirror, blocks, *scratch):
    a_ref, z_ref, linv_ref, d_ref, e_ref, first, second, reduced, came, grams, send, recv, tsend, trecv = scratch
    size = first.shape[0]
    height = factor.shape[0]
    mine = my_rows(height)
    enter([{"tm": wrap("tm", 1)}, {"tm": wrap("tm", -1)}])

    def over(i, by, src, dst):
        return pltpu.make_async_remote_copy(
            src_ref=src,
            dst_ref=dst,
            send_sem=tsend.at[i],
            recv_sem=trecv.at[i],
            device_id={"tm": wrap("tm", by)},
            device_id_type=MESH,
        )

    over_gram = over(0, 1, rgram, came.at[0])
    over_upper = over(1, 1, upper, first.at[mine])
    over_gram.start()
    over_upper.start()
    kept = diag[0] - lgram[...]
    second[mine, :] = mirror[...]
    blocks[1] = factor[...]
    a_ref[size + height:, :] = mirror[...]
    over_gram.wait_recv()
    reduced[...] = kept - came[0]
    pivot = [(reduced, a_ref.at[pl.ds(0, size)], send.at[0], recv.at[0])]
    couplings = [
        (first.at[mine], first, send.at[1], recv.at[1]),
        (mirror, second, send.at[2], recv.at[2]),
    ]
    gather_round(0, pivot)
    a_ref[mine, :] = reduced[...]
    over_upper.wait_recv()
    a_ref[size:size + height, :] = first[mine, :]
    for k in range(1, 4):
        gather_round(k, pivot)
    gather_round(0, couplings)
    gather_round(4, pivot)

    def during(j):
        if j < 3:
            gather_round(j + 1, couplings)

    reduce_block(size // NT, a_ref, z_ref, linv_ref, d_ref, e_ref, False, during)
    gather_round(4, couplings)
    over_gram.wait_send()
    over_upper.wait_send()
    for i, full in enumerate((first, second)):
        z = split(z_ref[i * height:(i + 1) * height, :])
        for n in range(0, size, 256):
            cols = slice(n, n + 256)
            grams[i, :, cols] = dot3(z, split(full[cols, :]), NTR)
    back = [over(2, -1, grams.at[0], came.at[1]), over(3, 1, grams.at[1], came.at[2])]
    for copy in back:
        copy.start()
    for copy in back:
        copy.wait()
    blocks[0] = reduced[...] - came[1] - came[2]


def call(kernel, outs, scratch, collective, *args):
    return pl.pallas_call(
        kernel,
        out_shape=[jax.ShapeDtypeStruct(s, F32) for s in outs],
        in_specs=[pl.BlockSpec(memory_space=pltpu.VMEM)] * len(args),
        out_specs=[pl.BlockSpec(memory_space=pltpu.VMEM)] * len(outs),
        scratch_shapes=scratch,
        compiler_params=pltpu.CompilerParams(
            vmem_limit_bytes=56 << 20, collective_id=collective, has_side_effects=True
        ),
    )(*args)


def solution(mesh):
    def shards(diag_blocks, left_blocks, right_blocks):
        height, size = left_blocks.shape[1:]
        part, full = (height, size), (size, size)
        sems = [pltpu.SemaphoreType.DMA((3, len(MESSAGES)))] * 2
        work = [
            pltpu.VMEM((size + 2 * height, size), F32),
            pltpu.VMEM((2 * height, size), F32),
            pltpu.VMEM((size // NT, NT, NT), F32),
            pltpu.VMEM((NT, NT), F32),
            pltpu.VMEM((NT, NT), F32),
            pltpu.VMEM(full, F32),
            pltpu.VMEM(full, F32),
        ]
        factor, solved, *rows = call(
            level_one,
            [part, (2, *part)] + [part] * 4,
            work + sems,
            0,
            diag_blocks,
            left_blocks[0],
            right_blocks[0],
        )
        extra = [pltpu.VMEM(part, F32), pltpu.VMEM((3, *part), F32), pltpu.VMEM((2, *part), F32)]
        over = [pltpu.SemaphoreType.DMA((4,))] * 2
        (blocks,) = call(
            level_two, [(2, *part)], work + extra + sems + over, 1, diag_blocks, factor, *rows
        )
        return blocks, solved[None]

    in_specs = (P("tm", "col", None), P("tm", "col", None), P("tm", "col", None))
    out_specs = (P("tm", "col", None), P("tm", None, "col", None))
    return jax.shard_map(shards, mesh=mesh, in_specs=in_specs, out_specs=out_specs, check_vma=False)
```

time: 304 us -> 159 us (0.52)
  Pallas kernels: 299 us -> 155 us
    pallas_call x5 -> x2, Pallas kernels: 299 us -> 155 us  [call(): pl.pallas_call(kernel, out_shape=[jax.ShapeDtypeStruct(s, F32) for s in o...]
where the time goes in v2:
time: 159 us; the launch traced here: 158 us
  Pallas kernels  155 us (97%)
  local copies, waits for them, and re-layouts  2.46 us (2%)
    pallas_call x2, Pallas kernels, call(): pl.pallas_call(kernel, out_shape=[jax.ShapeDtypeStruct(s, F32) for s in o...  155 us

profile of v2, /device:TPU:1, one launch (start us, length us, event | category | flops | bytes accessed | tf_op | source)
XLA Modules:
  0.0 158.5 jit_solution(16379663609873319852)
XLA Ops:
  0.6 71.4 %shard_map.50 = (f32[48,768]{1,0:T(8,128)}, f32[2,48,768]{2,1,0:T(8,128)}, f32[48,768]{1,0:T(8,128)}, f32[48,768]{1,0:T(8,128)}, f32[48,768]{1,0:T(8,128)}, /*index=5*/f32[48,768]{1,0:T(8,128)}) custom-call(f32[2,48,768]{2,1,0:T(8,128)} %diag.3, f32[48,768]{1,0:T(8,128)} %bitcast.4, f32[48,768]{1,0:T(8,128)} %bitcast.5), custom_call_target="tpu_custom_call" | custom-call | tf_op jit(solution)/shard_map/pallas_call | solution.py:356
  72.0 84.0 %shard_map.51 = f32[2,48,768]{2,1,0:T(8,128)} custom-call(f32[2,48,768]{2,1,0:T(8,128)} %diag.3, f32[48,768]{1,0:T(8,128)} %get-tuple-element.8.factor, f32[48,768]{1,0:T(8,128)} %get-tuple-element.9.lgram, f32[48,768]{1,0:T(8,128)} %get-tuple-element.10.rgram, f32[48,768]{1,0:T(8,128)} %get-tuple-element.11.upper, f32[48,768]{1,0:T(8,128)} %get-tuple-element.12.mirror), custom_call_target="tpu_custom_call" | custom-call | tf_op jit(solution)/shard_map/pallas_call | solution.py:356
  156.0 0.0 copy-start
  156.0 1.7 %copy.7 = f32[2,48,768]{2,1,0:T(8,128)} copy(f32[2,48,768]{2,1,0:T(8,128)} %shard_map.51) | data formatting | bytes 589824
  157.8 0.0 copy-done
  157.8 0.7 copy.8
Async XLA Ops:
  156.0 1.8 %copy-start = (f32[2,48,768]{2,1,0:T(8,128)S(1)}, f32[2,48,768]{2,1,0:T(8,128)}, u32[]{:S(2)}) copy-start(f32[2,48,768]{2,1,0:T(8,128)} %get-tuple-element.13) | copy-start | bytes 884740

commit v3 on v2

v3 whole, which is shorter than its diff:
```python
import jax
import jax.numpy as jnp
from jax import lax
from jax.experimental import pallas as pl
from jax.experimental.pallas import tpu as pltpu
from jax.sharding import PartitionSpec as P

F32 = jnp.float32
BF16 = jnp.bfloat16
NT = 128
SIDE = 4
MESH = pl.DeviceIdType.MESH
NN = (((1,), (0,)), ((), ()))
NTR = (((1,), (1,)), ((), ()))
TN = (((0,), (0,)), ((), ()))


def split(x):
    hi = x.astype(BF16)
    lo = (x - hi.astype(F32)).astype(BF16)
    return hi, lo


def bdot(a, b, dims):
    return lax.dot_general(a, b, dims, preferred_element_type=F32)


def dot3(a, b, dims):
    ah, al = a
    bh, bl = b
    return bdot(ah, bh, dims) + (bdot(ah, bl, dims) + bdot(al, bh, dims))


def lane(rows, j):
    return jnp.broadcast_to(rows[:, j:j + 1], (8, NT))

def factor_diag(d_ref, e_ref, p_ref):
    row = lax.broadcasted_iota(jnp.int32, (NT, NT), 0)
    col = lax.broadcasted_iota(jnp.int32, (NT, NT), 1)
    e_ref[...] = jnp.where(row == col, 1.0, 0.0).astype(F32)
    strips = NT // 8
    for s in range(strips):
        b = 8 * s
        half = 64 * (s % 2)
        strip = d_ref[b:b + 8, :]
        for j in range(8):
            p_ref[half + 8 * j:half + 8 * j + 8, :] = lane(strip, b + j)
        p = {(i, j): p_ref[pl.ds(half + 8 * j + i, 8, stride=0), :] for i in range(8) for j in range(i + 1)}
        d = [d_ref[pl.ds(b + i, 8, stride=0), :] for i in range(8)]
        e = [e_ref[pl.ds(b + i, 8, stride=0), :] for i in range(8)]
        more = s + 1 < strips
        if more:
            nd = d_ref[b + 8:b + 16, :]
            ne = e_ref[b + 8:b + 16, :]
            t = [lane(nd, b + k) for k in range(8)]
        for k in range(8):
            r = lax.rsqrt(p[k, k])
            for i in range(k + 1, 8):
                p[i, k] = p[i, k] * r
            for i in range(k + 1, 8):
                for j in range(k + 1, i + 1):
                    p[i, j] = p[i, j] - p[i, k] * p[j, k]
            d[k] = d[k] * r
            e[k] = e[k] * r
            for i in range(k + 1, 8):
                d[i] = d[i] - p[i, k] * d[k]
                e[i] = e[i] - p[i, k] * e[k]
            d_ref[b + k:b + k + 1, :] = d[k][:1]
            e_ref[b + k:b + k + 1, :] = e[k][:1]
            if more:
                t[k] = t[k] * r
                for i in range(k + 1, 8):
                    t[i] = t[i] - p[i, k] * t[k]
                nd = nd - t[k] * d[k]
                ne = ne - t[k] * e[k]
        if more:
            d_ref[b + 8:b + 16, :] = nd
            e_ref[b + 8:b + 16, :] = ne
        if s + 2 < strips:
            lo_row = b + 16
            w = jnp.concatenate([d_ref[b:b + 8, :], e_ref[b:b + 8, :]], axis=1)
            wh = w.astype(BF16).astype(F32)
            wl = w - wh
            rhs = jnp.concatenate([wh, wl, wh, wl], axis=0).astype(BF16)
            uh, ul = wh[:, :NT], wl[:, :NT]
            lhs = jnp.concatenate([uh, uh, ul, ul], axis=0).astype(BF16)
            upd = bdot(lhs, rhs, TN)[lo_row:, :]
            d_ref[lo_row:, :] = d_ref[lo_row:, :] - upd[:, :NT]
            e_ref[lo_row:, :] = e_ref[lo_row:, :] - upd[:, NT:]


def reduce_block(a_ref, z_ref, linv_ref, d_ref, e_ref, p_ref, keep_factor, during):
    size = a_ref.shape[1]
    blocks = size // NT
    rows = a_ref.shape[0]

    def step(j, carry):
        at = pl.ds(pl.multiple_of(j * NT, NT), NT)
        d_ref[...] = a_ref[at, at]
        factor_diag(d_ref, e_ref, p_ref)
        linv_ref[j] = e_ref[...]
        if keep_factor:
            a_ref[at, at] = d_ref[...].T
        for i in range(blocks):

            @pl.when(j == i)
            def _():
                during(i)
                cols = slice(i * NT, (i + 1) * NT)
                below = (i + 1) * NT
                panel = dot3(split(a_ref[below:, cols]), split(e_ref[...]), NTR)
                a_ref[below:, cols] = panel
                ph, pw = split(a_ref[below:, :below] if i == 1 else panel)
                for k in range(i + 1, 2 if i == 0 else blocks):
                    r = k * NT
                    o = r - below
                    new = dot3((ph[o:], pw[o:]), (ph[o:o + NT], pw[o:o + NT]), NTR)
                    a_ref[r:, r:r + NT] = a_ref[r:, r:r + NT] - new

        return carry

    lax.fori_loop(0, blocks, step, 0)
    for i in reversed(range(blocks)):
        cols = slice(i * NT, (i + 1) * NT)
        below = (i + 1) * NT
        acc = a_ref[size:rows, cols]
        if below < size:
            acc = acc - dot3(split(z_ref[:, below:]), split(a_ref[below:size, cols]), NN)
        z_ref[:, cols] = dot3(split(acc), split(linv_ref[i]), NN)


def wrap(axis, by):
    size = lax.axis_size(axis)
    return lax.rem(lax.axis_index(axis) + (by + size), size)


def plus(a, b):
    return (a[0] + b[0], a[1] + b[1])


def times(k, a):
    return (k * a[0], k * a[1])


RINGS = ((0, 1), (1, 0))
WHOLE, TOP, BOTTOM = (0, 2), (0, 1), (1, 2)


def relay_plan():
    messages, rounds = [], []

    def leave(towards, block, rows, part):
        messages.append((towards, block, rows, part))
        return len(messages) - 1

    def relay(axis, block, part):
        return [
            leave(axis, plus(block, times(-1, axis)), TOP, part),
            leave(times(-1, axis), plus(block, axis), BOTTOM, part),
        ]

    def both(axis, block, part):
        return [leave(axis, block, WHOLE, part), leave(times(-1, axis), block, WHOLE, part)]

    own = [m for axis in RINGS for m in both(axis, (0, 0), None)]
    rounds.append(([], own))
    far, sides, starts = [], [], []
    for part in range(2):
        a, b = RINGS[part], RINGS[1 - part]
        far.append(relay(a, (0, 0), part))
        sides.append([both(b, times(-1, a), part), both(b, a, part)])
        starts += far[part] + sides[part][0] + sides[part][1] + relay(b, (0, 0), part)
    rounds.append((own, starts))
    comes, starts, last = [], [], []
    for part in range(2):
        a, b = RINGS[part], RINGS[1 - part]
        comes += far[part] + sides[part][0] + sides[part][1]
        last.append(both(b, times(2, a), part))
        starts += last[part] + relay(b, times(-1, a), part) + relay(b, a, part)
    rounds.append((comes, starts))
    starts = []
    for part in range(2):
        a, b = RINGS[part], RINGS[1 - part]
        starts += relay(b, times(2, a), part)
    rounds.append((last[0] + last[1], starts))
    seen = {m for came, _ in rounds for m in came}
    rounds.append(([m for m in range(len(messages)) if m not in seen], []))
    return messages, rounds


def direct_plan():
    messages, starts = [], []
    hops = [[axis, times(-1, axis), times(2, axis)] for axis in RINGS]
    for ring in hops:
        for hop in ring:
            messages.append((hop, (0, 0), WHOLE, None))
    own = list(range(len(messages)))
    for part in range(2):
        for hop in hops[part]:
            for onward in hops[1 - part]:
                starts.append(len(messages))
                messages.append((onward, times(-1, hop), WHOLE, part))
    return messages, [([], own), (own, starts), (starts, [])]


RELAY, DIRECT = relay_plan(), direct_plan()
SLOTS = max(len(RELAY[0]), len(DIRECT[0]))


def col_device(by):
    me = lax.axis_index("col")
    y, x = lax.div(me, SIDE), lax.rem(me, SIDE)
    return lax.rem(y + (by[0] + SIDE), SIDE) * SIDE + lax.rem(x + (by[1] + SIDE), SIDE)


def gather_round(plan, k, *arrays):
    messages, rounds = plan

    def message(i, src, full, cols, send, recv):
        towards, block, rows, part = messages[i]
        height = full.shape[0] // SIDE**2
        begin, length = rows[0] * height // 2, (rows[1] - rows[0]) * height // 2
        at = pl.ds(pl.multiple_of(col_device(block) * height + begin, 8), length)
        half = (cols[1] - cols[0]) // 2
        over = pl.ds(*((cols[0], 2 * half) if part is None else (cols[0] + part * half, half)))
        there = full.at[at, over]
        return pltpu.make_async_remote_copy(
            src_ref=src.at[:, over] if block == (0, 0) and part is None else there,
            dst_ref=there,
            send_sem=send.at[i],
            recv_sem=recv.at[i],
            device_id={"col": col_device(towards)},
            device_id_type=MESH,
        )

    comes, starts = rounds[k]
    for array in arrays:
        for i in comes:
            message(i, *array).wait_recv()
    for array in arrays:
        for i in starts:
            message(i, *array).start()
    if k == len(rounds) - 1:
        for array in arrays:
            for i in range(len(messages)):
                message(i, *array).wait_send()


def enter(others):
    peers = [{"col": col_device(times(k, axis))} for axis in RINGS for k in (1, -1, 2)] + others
    barrier = pltpu.get_barrier_semaphore()
    for peer in peers:
        pl.semaphore_signal(barrier, inc=1, device_id=peer, device_id_type=MESH)
    pl.semaphore_wait(barrier, len(peers))


def kernel(diag, left, right, blocks, solved, *scratch):
    (a_one, a_two, left_full, right_full, first, second, z_ref, linv_ref, d_ref, e_ref, p_ref) = scratch[:11]
    (lgram, rgram, upper, mirror, reduced, came, grams, send, recv, tsend, trecv) = scratch[11:]
    height, size = left.shape
    near, rest = (0, 2 * NT), (2 * NT, size)
    mine = pl.ds(pl.multiple_of(lax.axis_index("col") * height, 16), height)
    enter([{"tm": wrap("tm", 1)}, {"tm": wrap("tm", -1)}])

    def factor(level, a_ref, pivot_rows, first_rows, second_rows, first_full, second_full, ready):
        full = a_ref.at[pl.ds(0, size)]
        sems = [(send.at[level, i], recv.at[level, i]) for i in range(4)]
        head = (pivot_rows, full, near, *sems[0])
        tail = (pivot_rows, full, rest, *sems[1])
        couplings = [
            (first_rows, first_full, (0, size), *sems[2]),
            (second_rows, second_full, (0, size), *sems[3]),
        ]
        gather_round(DIRECT, 1, head)
        a_ref[mine, :] = pivot_rows[...]
        ready()
        gather_round(DIRECT, 1, tail)
        gather_round(RELAY, 0, *couplings)
        gather_round(DIRECT, 2, head)

        def during(j):
            if j == 1:
                gather_round(DIRECT, 2, tail)
            if j < 3:
                gather_round(RELAY, j + 1, *couplings)

        reduce_block(a_ref, z_ref, linv_ref, d_ref, e_ref, p_ref, level == 0, during)
        gather_round(RELAY, 4, *couplings)

    def begin(level, a_ref, pivot_rows, cols):
        i = 0 if cols == near else 1
        gather_round(
            DIRECT, 0, (pivot_rows, a_ref.at[pl.ds(0, size)], cols, send.at[level, i], recv.at[level, i])
        )

    def over(i, by, src, dst):
        return pltpu.make_async_remote_copy(
            src_ref=src,
            dst_ref=dst,
            send_sem=tsend.at[i],
            recv_sem=trecv.at[i],
            device_id={"tm": wrap("tm", by)},
            device_id_type=MESH,
        )

    odd = diag.at[1]
    begin(0, a_one, odd, near)
    begin(0, a_one, odd, rest)

    def ready_one():
        a_one[size:size + height, :] = left[...]
        a_one[size + height:, :] = right[...]
        left_full[mine, :] = left[...]
        right_full[mine, :] = right[...]

    factor(0, a_one, odd, left, right, left_full, right_full, ready_one)

    z = split(z_ref[...])
    head_gram = over(0, 1, rgram.at[:, pl.ds(0, 2 * NT)], came.at[0, :, pl.ds(0, 2 * NT)])
    tail_gram = over(1, 1, rgram.at[:, pl.ds(2 * NT, size - 2 * NT)], came.at[0, :, pl.ds(2 * NT, size - 2 * NT)])
    over_upper = over(2, 1, upper, first.at[mine])

    def with_right(cols):
        both = dot3(z, split(right_full[cols, :]), NTR)
        upper[:, cols] = -both[:height]
        rgram[:, cols] = both[height:]

    def with_left(cols):
        both = dot3(z, split(left_full[cols, :]), NTR)
        lgram[:, cols] = both[:height]
        mirror[:, cols] = -both[height:]

    parts = [slice(n, n + 2 * NT) for n in range(0, size, 2 * NT)]
    with_right(parts[0])
    head_gram.start()
    for cols in parts[1:]:
        with_right(cols)
    tail_gram.start()
    over_upper.start()
    with_left(parts[0])
    head_gram.wait_recv()
    reduced[:, parts[0]] = diag[0, :, parts[0]] - lgram[:, parts[0]] - came[0, :, parts[0]]
    begin(1, a_two, reduced, near)
    for cols in parts[1:]:
        with_left(cols)
    tail_gram.wait_recv()
    reduced[:, 2 * NT:] = diag[0, :, 2 * NT:] - lgram[:, 2 * NT:] - came[0, :, 2 * NT:]
    begin(1, a_two, reduced, rest)
    row = lax.axis_index("col") * height + lax.broadcasted_iota(jnp.int32, (height, size), 0)
    col = lax.broadcasted_iota(jnp.int32, (height, size), 1)
    blocks[1] = jnp.where(col <= row, a_one[mine, :], 0.0)
    solved[0] = a_one[size:size + height, :]
    solved[1] = a_one[size + height:, :]

    def ready_two():
        second[mine, :] = mirror[...]
        a_two[size + height:, :] = mirror[...]
        over_upper.wait_recv()
        a_two[size:size + height, :] = first[mine, :]

    factor(1, a_two, reduced, first.at[mine], mirror, first, second, ready_two)

    zs = [split(z_ref[i * height:(i + 1) * height, :]) for i in range(2)]
    back = []
    for n, cols in enumerate(parts):
        there = pl.ds(n * 2 * NT, 2 * NT)
        for i, (full, by) in enumerate(((first, -1), (second, 1))):
            grams[i, :, cols] = dot3(zs[i], split(full[cols, :]), NTR)
            back.append(over(3 + 2 * n + i, by, grams.at[i, :, there], came.at[1 + i, :, there]))
            back[-1].start()
    for copy in (head_gram, tail_gram, over_upper):
        copy.wait_send()
    for copy in back:
        copy.wait()
    blocks[0] = reduced[...] - came[1] - came[2]


def solution(mesh):
    def shards(diag_blocks, left_blocks, right_blocks):
        height, size = left_blocks.shape[1:]
        part, full = (height, size), (size, size)
        tall = (size + 2 * height, size)
        shapes = [tall, tall, full, full, full, full, (2 * height, size), (size // NT, NT, NT)]
        shapes += [(NT, NT)] * 3 + [part] * 5 + [(3, *part), (2, *part)]
        sems = [pltpu.SemaphoreType.DMA((2, 4, SLOTS))] * 2 + [pltpu.SemaphoreType.DMA((16,))] * 2
        blocks, solved = pl.pallas_call(
            kernel,
            out_shape=[jax.ShapeDtypeStruct((2, *part), F32)] * 2,
            in_specs=[pl.BlockSpec(memory_space=pltpu.VMEM)] * 3,
            out_specs=[pl.BlockSpec(memory_space=pltpu.VMEM)] * 2,
            scratch_shapes=[pltpu.VMEM(s, F32) for s in shapes] + sems,
            compiler_params=pltpu.CompilerParams(
                vmem_limit_bytes=56 << 20, collective_id=0, has_side_effects=True
            ),
        )(diag_blocks, left_blocks[0], right_blocks[0])
        return blocks, solved[None]

    in_specs = (P("tm", "col", None), P("tm", "col", None), P("tm", "col", None))
    out_specs = (P("tm", "col", None), P("tm", None, "col", None))
    return jax.shard_map(shards, mesh=mesh, in_specs=in_specs, out_specs=out_specs, check_vma=False)
```

time: 159 us -> 144 us (0.906)
  Pallas kernels: 155 us -> 140 us
    pallas_call x2 -> x1, Pallas kernels: 155 us -> 140 us  [shards(): pl.pallas_call(kernel, out_shape=[jax.ShapeDtypeStruct((2, *part), F32)]...]
where the time goes in v3:
time: 144 us; the launch traced here: 143 us
  Pallas kernels  140 us (97%)
  local copies, waits for them, and re-layouts  2.46 us (2%)
    pallas_call x1, Pallas kernels, shards(): pl.pallas_call(kernel, out_shape=[jax.ShapeDtypeStruct((2, *part), F32)]...  140 us

profile of v3, /device:TPU:1, one launch (start us, length us, event | category | flops | bytes accessed | tf_op | source)
XLA Modules:
  0.0 142.8 jit_solution(453674959263153253)
XLA Ops:
  0.6 139.7 %shard_map.50 = (f32[2,48,768]{2,1,0:T(8,128)}, f32[2,48,768]{2,1,0:T(8,128)}) custom-call(f32[2,48,768]{2,1,0:T(8,128)} %diag.1, f32[48,768]{1,0:T(8,128)} %bitcast.4, f32[48,768]{1,0:T(8,128)} %bitcast.5), custom_call_target="tpu_custom_call" | custom-call | tf_op jit(solution)/shard_map/pallas_call | solution.py:386
  140.3 0.0 copy-start
  140.3 1.7 %copy.7 = f32[2,48,768]{2,1,0:T(8,128)} copy(f32[2,48,768]{2,1,0:T(8,128)} %get-tuple-element.8) | data formatting | bytes 589824
  142.0 0.0 copy-done
  142.0 0.7 copy.8
Async XLA Ops:
  140.3 1.8 %copy-start = (f32[2,48,768]{2,1,0:T(8,128)S(1)}, f32[2,48,768]{2,1,0:T(8,128)}, u32[]{:S(2)}) copy-start(f32[2,48,768]{2,1,0:T(8,128)} %get-tuple-element.5) | copy-start | bytes 884740

commit v4 on v3

--- a/solution.py
+++ b/solution.py
@@ -204,6 +204,9 @@
 
 
 RELAY, DIRECT = relay_plan(), direct_plan()
+START = 1
+EARLY_AT = (1, 3)
+LATE_AT = (0, 2, 4)
 SLOTS = max(len(RELAY[0]), len(DIRECT[0]))
 
 
@@ -216,7 +219,7 @@
 def gather_round(plan, k, *arrays):
     messages, rounds = plan
 
-    def message(i, src, full, cols, send, recv):
+    def message(i, src, full, cols, lowest, send, recv):
         towards, block, rows, part = messages[i]
         height = full.shape[0] // SIDE**2
         begin, length = rows[0] * height // 2, (rows[1] - rows[0]) * height // 2
@@ -233,17 +236,21 @@
             device_id_type=MESH,
         )
 
+    def each(indices, act, seen_from_here):
+        for array in arrays:
+            for i in indices:
+                towards, block = messages[i][:2]
+                moved = block if seen_from_here else plus(block, times(-1, towards))
+                if array[3] == 0:
+                    act(message(i, *array))
+                else:
+                    pl.when(col_device(moved) >= array[3])(lambda: act(message(i, *array)))
+
     comes, starts = rounds[k]
-    for array in arrays:
-        for i in comes:
-            message(i, *array).wait_recv()
-    for array in arrays:
-        for i in starts:
-            message(i, *array).start()
+    each(comes, lambda copy: copy.wait_recv(), False)
+    each(starts, lambda copy: copy.start(), True)
     if k == len(rounds) - 1:
-        for array in arrays:
-            for i in range(len(messages)):
-                message(i, *array).wait_send()
+        each(range(len(messages)), lambda copy: copy.wait_send(), True)
 
 
 def enter(others):
@@ -262,36 +269,40 @@
     mine = pl.ds(pl.multiple_of(lax.axis_index("col") * height, 16), height)
     enter([{"tm": wrap("tm", 1)}, {"tm": wrap("tm", -1)}])
 
-    def factor(level, a_ref, pivot_rows, first_rows, second_rows, first_full, second_full, ready):
+    def factor(level, a_ref, pivot_rows, early_rows, early_full, late_rows, late_full, ready):
         full = a_ref.at[pl.ds(0, size)]
         sems = [(send.at[level, i], recv.at[level, i]) for i in range(4)]
-        head = (pivot_rows, full, near, *sems[0])
-        tail = (pivot_rows, full, rest, *sems[1])
-        couplings = [
-            (first_rows, first_full, (0, size), *sems[2]),
-            (second_rows, second_full, (0, size), *sems[3]),
-        ]
+        head = (pivot_rows, full, near, 0, *sems[0])
+        tail = (pivot_rows, full, rest, 2 * NT // height, *sems[1])
+        early = (early_rows, early_full, (0, size), 0, *sems[2])
+        late = (late_rows, late_full, (0, size), 0, *sems[3])
         gather_round(DIRECT, 1, head)
+        gather_round(DIRECT, 0, tail)
         a_ref[mine, :] = pivot_rows[...]
         ready()
+        gather_round(RELAY, 0, late)
+        gather_round(DIRECT, 2, head)
         gather_round(DIRECT, 1, tail)
-        gather_round(RELAY, 0, *couplings)
-        gather_round(DIRECT, 2, head)
+        if START:
+            gather_round(RELAY, 1, early)
 
         def during(j):
             if j == 1:
                 gather_round(DIRECT, 2, tail)
-            if j < 3:
-                gather_round(RELAY, j + 1, *couplings)
+            if j in EARLY_AT:
+                gather_round(RELAY, START + 1 + EARLY_AT.index(j), early)
+            if j in LATE_AT:
+                gather_round(RELAY, 1 + LATE_AT.index(j), late)
 
         reduce_block(a_ref, z_ref, linv_ref, d_ref, e_ref, p_ref, level == 0, during)
-        gather_round(RELAY, 4, *couplings)
-
-    def begin(level, a_ref, pivot_rows, cols):
-        i = 0 if cols == near else 1
-        gather_round(
-            DIRECT, 0, (pivot_rows, a_ref.at[pl.ds(0, size)], cols, send.at[level, i], recv.at[level, i])
-        )
+        gather_round(RELAY, 4, early, late)
+
+    def begin(level, a_ref, pivot_rows):
+        full = a_ref.at[pl.ds(0, size)]
+        gather_round(DIRECT, 0, (pivot_rows, full, near, 0, send.at[level, 0], recv.at[level, 0]))
+
+    def begin_early(level, rows, full):
+        gather_round(RELAY, 0, (rows, full, (0, size), 0, send.at[level, 2], recv.at[level, 2]))
 
     def over(i, by, src, dst):
         return pltpu.make_async_remote_copy(
@@ -304,8 +315,8 @@
         )
 
     odd = diag.at[1]
-    begin(0, a_one, odd, near)
-    begin(0, a_one, odd, rest)
+    begin(0, a_one, odd)
+    begin_early(0, left, left_full)
 
     def ready_one():
         a_one[size:size + height, :] = left[...]
@@ -313,7 +324,7 @@
         left_full[mine, :] = left[...]
         right_full[mine, :] = right[...]
 
-    factor(0, a_one, odd, left, right, left_full, right_full, ready_one)
+    factor(0, a_one, odd, left, left_full, right, right_full, ready_one)
 
     z = split(z_ref[...])
     head_gram = over(0, 1, rgram.at[:, pl.ds(0, 2 * NT)], came.at[0, :, pl.ds(0, 2 * NT)])
@@ -340,12 +351,12 @@
     with_left(parts[0])
     head_gram.wait_recv()
     reduced[:, parts[0]] = diag[0, :, parts[0]] - lgram[:, parts[0]] - came[0, :, parts[0]]
-    begin(1, a_two, reduced, near)
+    begin(1, a_two, reduced)
     for cols in parts[1:]:
         with_left(cols)
+    begin_early(1, mirror, second)
     tail_gram.wait_recv()
     reduced[:, 2 * NT:] = diag[0, :, 2 * NT:] - lgram[:, 2 * NT:] - came[0, :, 2 * NT:]
-    begin(1, a_two, reduced, rest)
     row = lax.axis_index("col") * height + lax.broadcasted_iota(jnp.int32, (height, size), 0)
     col = lax.broadcasted_iota(jnp.int32, (height, size), 1)
     blocks[1] = jnp.where(col <= row, a_one[mine, :], 0.0)
@@ -358,7 +369,7 @@
         over_upper.wait_recv()
         a_two[size:size + height, :] = first[mine, :]
 
-    factor(1, a_two, reduced, first.at[mine], mirror, first, second, ready_two)
+    factor(1, a_two, reduced, mirror, second, first.at[mine], first, ready_two)
 
     zs = [split(z_ref[i * height:(i + 1) * height, :]) for i in range(2)]
     back = []

time: 144 us -> 130 us (0.903)
  Pallas kernels: 140 us -> 126 us
    pallas_call x1, Pallas kernels: 140 us -> 126 us  [shards(): pl.pallas_call(kernel, out_shape=[jax.ShapeDtypeStruct((2, *part), F32)]...]
where the time goes in v4:
time: 130 us; the launch traced here: 129 us
  Pallas kernels  126 us (97%)
  local copies, waits for them, and re-layouts  2.46 us (2%)
    pallas_call x1, Pallas kernels, shards(): pl.pallas_call(kernel, out_shape=[jax.ShapeDtypeStruct((2, *part), F32)]...  126 us

profile of v4, /device:TPU:1, one launch (start us, length us, event | category | flops | bytes accessed | tf_op | source)
XLA Modules:
  0.0 129.3 jit_solution(7898698838980866974)
XLA Ops:
  0.6 126.2 %shard_map.50 = (f32[2,48,768]{2,1,0:T(8,128)}, f32[2,48,768]{2,1,0:T(8,128)}) custom-call(f32[2,48,768]{2,1,0:T(8,128)} %diag.1, f32[48,768]{1,0:T(8,128)} %bitcast.4, f32[48,768]{1,0:T(8,128)} %bitcast.5), custom_call_target="tpu_custom_call" | custom-call | tf_op jit(solution)/shard_map/pallas_call | solution.py:397
  126.9 0.0 copy-start
  126.9 1.7 %copy.7 = f32[2,48,768]{2,1,0:T(8,128)} copy(f32[2,48,768]{2,1,0:T(8,128)} %get-tuple-element.8) | data formatting | bytes 589824
  128.6 0.0 copy-done
  128.6 0.7 copy.8
Async XLA Ops:
  126.9 1.8 %copy-start = (f32[2,48,768]{2,1,0:T(8,128)S(1)}, f32[2,48,768]{2,1,0:T(8,128)}, u32[]{:S(2)}) copy-start(f32[2,48,768]{2,1,0:T(8,128)} %get-tuple-element.5) | copy-start | bytes 884740

commit v5 on v4

--- a/solution.py
+++ b/solution.py
@@ -34,7 +34,7 @@
 def lane(rows, j):
     return jnp.broadcast_to(rows[:, j:j + 1], (8, NT))
 
-def factor_diag(d_ref, e_ref, p_ref):
+def factor_diag(d_ref, e_ref, p_ref, q_ref):
     row = lax.broadcasted_iota(jnp.int32, (NT, NT), 0)
     col = lax.broadcasted_iota(jnp.int32, (NT, NT), 1)
     e_ref[...] = jnp.where(row == col, 1.0, 0.0).astype(F32)
@@ -43,16 +43,19 @@
         b = 8 * s
         half = 64 * (s % 2)
         strip = d_ref[b:b + 8, :]
-        for j in range(8):
-            p_ref[half + 8 * j:half + 8 * j + 8, :] = lane(strip, b + j)
+        if s == 0:
+            for j in range(8):
+                p_ref[half + 8 * j:half + 8 * j + 8, :] = lane(strip, b + j)
         p = {(i, j): p_ref[pl.ds(half + 8 * j + i, 8, stride=0), :] for i in range(8) for j in range(i + 1)}
         d = [d_ref[pl.ds(b + i, 8, stride=0), :] for i in range(8)]
         e = [e_ref[pl.ds(b + i, 8, stride=0), :] for i in range(8)]
-        more = s + 1 < strips
-        if more:
-            nd = d_ref[b + 8:b + 16, :]
-            ne = e_ref[b + 8:b + 16, :]
-            t = [lane(nd, b + k) for k in range(8)]
+        ahead = range(s + 1, min(strips, s + GROUP - s % GROUP + LOOK))
+        nd = {q: d_ref[8 * q:8 * q + 8, :] for q in ahead}
+        ne = {q: e_ref[8 * q:8 * q + 8, :] for q in ahead}
+        t = {q: [lane(nd[q], b + k) for k in range(8)] for q in ahead}
+        nxt = s + 1 < strips
+        if nxt:
+            c = [lane(nd[s + 1], b + 8 + j) for j in range(8)]
         for k in range(8):
             r = lax.rsqrt(p[k, k])
             for i in range(k + 1, 8):
@@ -67,18 +70,27 @@
                 e[i] = e[i] - p[i, k] * e[k]
             d_ref[b + k:b + k + 1, :] = d[k][:1]
             e_ref[b + k:b + k + 1, :] = e[k][:1]
-            if more:
-                t[k] = t[k] * r
+            for q in ahead:
+                t[q][k] = t[q][k] * r
                 for i in range(k + 1, 8):
-                    t[i] = t[i] - p[i, k] * t[k]
-                nd = nd - t[k] * d[k]
-                ne = ne - t[k] * e[k]
-        if more:
-            d_ref[b + 8:b + 16, :] = nd
-            e_ref[b + 8:b + 16, :] = ne
-        if s + 2 < strips:
-            lo_row = b + 16
-            w = jnp.concatenate([d_ref[b:b + 8, :], e_ref[b:b + 8, :]], axis=1)
+                    t[q][i] = t[q][i] - p[i, k] * t[q][k]
+                nd[q] = nd[q] - t[q][k] * d[k]
+                ne[q] = ne[q] - t[q][k] * e[k]
+            if nxt:
+                q_ref[half + 8 * k:half + 8 * k + 8, :] = t[s + 1][k]
+                for j in range(8):
+                    c[j] = c[j] - t[s + 1][k] * q_ref[pl.ds(half + 8 * k + j, 8, stride=0), :]
+        if nxt:
+            for j in range(8):
+                p_ref[64 - half + 8 * j:64 - half + 8 * j + 8, :] = c[j]
+        for q in ahead:
+            d_ref[8 * q:8 * q + 8, :] = nd[q]
+            e_ref[8 * q:8 * q + 8, :] = ne[q]
+        far = s + 1 + LOOK
+        if s % GROUP == GROUP - 1 and far < strips:
+            lo_row = 8 * far
+            top = b + 8 - 8 * GROUP
+            w = jnp.concatenate([d_ref[top:b + 8, :], e_ref[top:b + 8, :]], axis=1)
             wh = w.astype(BF16).astype(F32)
             wl = w - wh
             rhs = jnp.concatenate([wh, wl, wh, wl], axis=0).astype(BF16)
@@ -89,7 +101,7 @@
             e_ref[lo_row:, :] = e_ref[lo_row:, :] - upd[:, NT:]
 
 
-def reduce_block(a_ref, z_ref, linv_ref, d_ref, e_ref, p_ref, keep_factor, during):
+def reduce_block(a_ref, z_ref, linv_ref, d_ref, e_ref, p_ref, q_ref, keep_factor, during):
     size = a_ref.shape[1]
     blocks = size // NT
     rows = a_ref.shape[0]
@@ -97,7 +109,7 @@
     def step(j, carry):
         at = pl.ds(pl.multiple_of(j * NT, NT), NT)
         d_ref[...] = a_ref[at, at]
-        factor_diag(d_ref, e_ref, p_ref)
+        factor_diag(d_ref, e_ref, p_ref, q_ref)
         linv_ref[j] = e_ref[...]
         if keep_factor:
             a_ref[at, at] = d_ref[...].T
@@ -205,8 +217,9 @@
 
 RELAY, DIRECT = relay_plan(), direct_plan()
 START = 1
-EARLY_AT = (1, 3)
-LATE_AT = (0, 2, 4)
+EARLY_AT = (2, 4)
+LATE_AT = (1, 3, 5)
+GROUP, LOOK = 2, 2
 SLOTS = max(len(RELAY[0]), len(DIRECT[0]))
 
 
@@ -262,8 +275,8 @@
 
 
 def kernel(diag, left, right, blocks, solved, *scratch):
-    (a_one, a_two, left_full, right_full, first, second, z_ref, linv_ref, d_ref, e_ref, p_ref) = scratch[:11]
-    (lgram, rgram, upper, mirror, reduced, came, grams, send, recv, tsend, trecv) = scratch[11:]
+    (a_one, a_two, left_full, right_full, first, second, z_ref, linv_ref, d_ref, e_ref, p_ref, q_ref) = scratch[:12]
+    (lgram, rgram, upper, mirror, reduced, came, grams, send, recv, tsend, trecv) = scratch[12:]
     height, size = left.shape
     near, rest = (0, 2 * NT), (2 * NT, size)
     mine = pl.ds(pl.multiple_of(lax.axis_index("col") * height, 16), height)
@@ -294,7 +307,7 @@
             if j in LATE_AT:
                 gather_round(RELAY, 1 + LATE_AT.index(j), late)
 
-        reduce_block(a_ref, z_ref, linv_ref, d_ref, e_ref, p_ref, level == 0, during)
+        reduce_block(a_ref, z_ref, linv_ref, d_ref, e_ref, p_ref, q_ref, level == 0, during)
         gather_round(RELAY, 4, early, late)
 
     def begin(level, a_ref, pivot_rows):
@@ -392,7 +405,7 @@
         part, full = (height, size), (size, size)
         tall = (size + 2 * height, size)
         shapes = [tall, tall, full, full, full, full, (2 * height, size), (size // NT, NT, NT)]
-        shapes += [(NT, NT)] * 3 + [part] * 5 + [(3, *part), (2, *part)]
+        shapes += [(NT, NT)] * 4 + [part] * 5 + [(3, *part), (2, *part)]
         sems = [pltpu.SemaphoreType.DMA((2, 4, SLOTS))] * 2 + [pltpu.SemaphoreType.DMA((16,))] * 2
         blocks, solved = pl.pallas_call(
             kernel,

time: 130 us -> 119 us (0.915)
  Pallas kernels: 126 us -> 116 us
    pallas_call x1, Pallas kernels: 126 us -> 116 us  [shards(): pl.pallas_call(kernel, out_shape=[jax.ShapeDtypeStruct((2, *part), F32)]...]
where the time goes in v5:
time: 119 us
  Pallas kernels  116 us (97%)
  local copies, waits for them, and re-layouts  2.46 us (2%)
    pallas_call x1, Pallas kernels, shards(): pl.pallas_call(kernel, out_shape=[jax.ShapeDtypeStruct((2, *part), F32)]...  116 us
    unnamed x4, local copies, waits for them, and re-layouts  2.46 us

profile of v5, /device:TPU:1, one launch (start us, length us, event | category | flops | bytes accessed | tf_op | source)
XLA Modules:
  0.0 119.1 jit_solution(4822001510321291409)
XLA Ops:
  0.6 116.0 %shard_map.50 = (f32[2,48,768]{2,1,0:T(8,128)}, f32[2,48,768]{2,1,0:T(8,128)}) custom-call(f32[2,48,768]{2,1,0:T(8,128)} %diag.1, f32[48,768]{1,0:T(8,128)} %bitcast.4, f32[48,768]{1,0:T(8,128)} %bitcast.5), custom_call_target="tpu_custom_call" | custom-call | tf_op jit(solution)/shard_map/pallas_call | solution.py:410
  116.6 0.0 copy-start
  116.6 1.7 %copy.7 = f32[2,48,768]{2,1,0:T(8,128)} copy(f32[2,48,768]{2,1,0:T(8,128)} %get-tuple-element.8) | data formatting | bytes 589824
  118.3 0.0 copy-done
  118.3 0.7 copy.8
Async XLA Ops:
  116.6 1.8 %copy-start = (f32[2,48,768]{2,1,0:T(8,128)S(1)}, f32[2,48,768]{2,1,0:T(8,128)}, u32[]{:S(2)}) copy-start(f32[2,48,768]{2,1,0:T(8,128)} %get-tuple-element.5) | copy-start | bytes 884740

commit v6 on v5

--- a/solution.py
+++ b/solution.py
@@ -175,26 +175,20 @@
         return [leave(axis, block, WHOLE, part), leave(times(-1, axis), block, WHOLE, part)]
 
     own = [m for axis in RINGS for m in both(axis, (0, 0), None)]
+    own += [leave(times(2, RINGS[part]), (0, 0), WHOLE, part) for part in range(2)]
     rounds.append(([], own))
-    far, sides, starts = [], [], []
+    sides, starts, relays = [], [], []
     for part in range(2):
         a, b = RINGS[part], RINGS[1 - part]
-        far.append(relay(a, (0, 0), part))
-        sides.append([both(b, times(-1, a), part), both(b, a, part)])
-        starts += far[part] + sides[part][0] + sides[part][1] + relay(b, (0, 0), part)
-    rounds.append((own, starts))
-    comes, starts, last = [], [], []
+        for hop in (a, times(-1, a), times(2, a)):
+            sides += both(b, hop, part)
+        starts += relay(b, (0, 0), part)
+    rounds.append((own, sides + starts))
     for part in range(2):
         a, b = RINGS[part], RINGS[1 - part]
-        comes += far[part] + sides[part][0] + sides[part][1]
-        last.append(both(b, times(2, a), part))
-        starts += last[part] + relay(b, times(-1, a), part) + relay(b, a, part)
-    rounds.append((comes, starts))
-    starts = []
-    for part in range(2):
-        a, b = RINGS[part], RINGS[1 - part]
-        starts += relay(b, times(2, a), part)
-    rounds.append((last[0] + last[1], starts))
+        for hop in (a, times(-1, a), times(2, a)):
+            relays += relay(b, hop, part)
+    rounds.append((sides, relays))
     seen = {m for came, _ in rounds for m in came}
     rounds.append(([m for m in range(len(messages)) if m not in seen], []))
     return messages, rounds
@@ -217,8 +211,8 @@
 
 RELAY, DIRECT = relay_plan(), direct_plan()
 START = 1
-EARLY_AT = (2, 4)
-LATE_AT = (1, 3, 5)
+EARLY_AT = (4,)
+LATE_AT = (3, 5)
 GROUP, LOOK = 2, 2
 SLOTS = max(len(RELAY[0]), len(DIRECT[0]))
 
@@ -241,7 +235,7 @@
         over = pl.ds(*((cols[0], 2 * half) if part is None else (cols[0] + part * half, half)))
         there = full.at[at, over]
         return pltpu.make_async_remote_copy(
-            src_ref=src.at[:, over] if block == (0, 0) and part is None else there,
+            src_ref=src.at[:, over] if block == (0, 0) and k == 0 else there,
             dst_ref=there,
             send_sem=send.at[i],
             recv_sem=recv.at[i],
@@ -293,9 +287,9 @@
         gather_round(DIRECT, 0, tail)
         a_ref[mine, :] = pivot_rows[...]
         ready()
-        gather_round(RELAY, 0, late)
         gather_round(DIRECT, 2, head)
         gather_round(DIRECT, 1, tail)
+        gather_round(RELAY, 0, late)
         if START:
             gather_round(RELAY, 1, early)
 
@@ -308,7 +302,8 @@
                 gather_round(RELAY, 1 + LATE_AT.index(j), late)
 
         reduce_block(a_ref, z_ref, linv_ref, d_ref, e_ref, p_ref, q_ref, level == 0, during)
-        gather_round(RELAY, 4, early, late)
+        gather_round(RELAY, 3, early)
+        return late
 
     def begin(level, a_ref, pivot_rows):
         full = a_ref.at[pl.ds(0, size)]
@@ -329,7 +324,7 @@
 
     odd = diag.at[1]
     begin(0, a_one, odd)
-    begin_early(0, left, left_full)
+    begin_early(0, right, right_full)
 
     def ready_one():
         a_one[size:size + height, :] = left[...]
@@ -337,7 +332,7 @@
         left_full[mine, :] = left[...]
         right_full[mine, :] = right[...]
 
-    factor(0, a_one, odd, left, left_full, right, right_full, ready_one)
+    late = factor(0, a_one, odd, right, right_full, left, left_full, ready_one)
 
     z = split(z_ref[...])
     head_gram = over(0, 1, rgram.at[:, pl.ds(0, 2 * NT)], came.at[0, :, pl.ds(0, 2 * NT)])
@@ -361,6 +356,7 @@
         with_right(cols)
     tail_gram.start()
     over_upper.start()
+    gather_round(RELAY, 3, late)
     with_left(parts[0])
     head_gram.wait_recv()
     reduced[:, parts[0]] = diag[0, :, parts[0]] - lgram[:, parts[0]] - came[0, :, parts[0]]
@@ -382,13 +378,15 @@
         over_upper.wait_recv()
         a_two[size:size + height, :] = first[mine, :]
 
-    factor(1, a_two, reduced, mirror, second, first.at[mine], first, ready_two)
+    late = factor(1, a_two, reduced, mirror, second, first.at[mine], first, ready_two)
 
     zs = [split(z_ref[i * height:(i + 1) * height, :]) for i in range(2)]
     back = []
-    for n, cols in enumerate(parts):
-        there = pl.ds(n * 2 * NT, 2 * NT)
-        for i, (full, by) in enumerate(((first, -1), (second, 1))):
+    for i, (full, by) in ((1, (second, 1)), (0, (first, -1))):
+        if i == 0:
+            gather_round(RELAY, 3, late)
+        for n, cols in enumerate(parts):
+            there = pl.ds(n * 2 * NT, 2 * NT)
             grams[i, :, cols] = dot3(zs[i], split(full[cols, :]), NTR)
             back.append(over(3 + 2 * n + i, by, grams.at[i, :, there], came.at[1 + i, :, there]))
             back[-1].start()

time: 119 us -> 115 us (0.966)
  Pallas kernels: 116 us -> 111 us
    pallas_call x1, Pallas kernels: 116 us -> 111 us  [shards(): pl.pallas_call(kernel, out_shape=[jax.ShapeDtypeStruct((2, *part), F32)]...]
where the time goes in v6:
time: 115 us; the launch traced here: 114 us
  Pallas kernels  111 us (97%)
  local copies, waits for them, and re-layouts  2.46 us (2%)
    pallas_call x1, Pallas kernels, shards(): pl.pallas_call(kernel, out_shape=[jax.ShapeDtypeStruct((2, *part), F32)]...  111 us
    unnamed x4, local copies, waits for them, and re-layouts  2.46 us

profile of v6, /device:TPU:1, one launch (start us, length us, event | category | flops | bytes accessed | tf_op | source)
XLA Modules:
  0.0 114.2 jit_solution(1608076694483535551)
XLA Ops:
  0.6 111.1 %shard_map.50 = (f32[2,48,768]{2,1,0:T(8,128)}, f32[2,48,768]{2,1,0:T(8,128)}) custom-call(f32[2,48,768]{2,1,0:T(8,128)} %diag.1, f32[48,768]{1,0:T(8,128)} %bitcast.4, f32[48,768]{1,0:T(8,128)} %bitcast.5), custom_call_target="tpu_custom_call" | custom-call | tf_op jit(solution)/shard_map/pallas_call | solution.py:408
  111.8 0.0 copy-start
  111.8 1.7 %copy.7 = f32[2,48,768]{2,1,0:T(8,128)} copy(f32[2,48,768]{2,1,0:T(8,128)} %get-tuple-element.8) | data formatting | bytes 589824
  113.5 0.0 copy-done
  113.5 0.7 copy.8
Async XLA Ops:
  111.8 1.8 %copy-start = (f32[2,48,768]{2,1,0:T(8,128)S(1)}, f32[2,48,768]{2,1,0:T(8,128)}, u32[]{:S(2)}) copy-start(f32[2,48,768]{2,1,0:T(8,128)} %get-tuple-element.5) | copy-start | bytes 884740

commit v7 on v6

--- a/solution.py
+++ b/solution.py
@@ -272,30 +272,30 @@
     (a_one, a_two, left_full, right_full, first, second, z_ref, linv_ref, d_ref, e_ref, p_ref, q_ref) = scratch[:12]
     (lgram, rgram, upper, mirror, reduced, came, grams, send, recv, tsend, trecv) = scratch[12:]
     height, size = left.shape
-    near, rest = (0, 2 * NT), (2 * NT, size)
+    near = (0, 2 * NT)
     mine = pl.ds(pl.multiple_of(lax.axis_index("col") * height, 16), height)
     enter([{"tm": wrap("tm", 1)}, {"tm": wrap("tm", -1)}])
 
     def factor(level, a_ref, pivot_rows, early_rows, early_full, late_rows, late_full, ready):
         full = a_ref.at[pl.ds(0, size)]
-        sems = [(send.at[level, i], recv.at[level, i]) for i in range(4)]
+        sems = [(send.at[level, i], recv.at[level, i]) for i in range(5)]
         head = (pivot_rows, full, near, 0, *sems[0])
-        tail = (pivot_rows, full, rest, 2 * NT // height, *sems[1])
+        tail = [(pivot_rows, full, (c, c + 2 * NT), c // height, *sems[i]) for c, i in ((2 * NT, 1), (4 * NT, 4))]
         early = (early_rows, early_full, (0, size), 0, *sems[2])
         late = (late_rows, late_full, (0, size), 0, *sems[3])
         gather_round(DIRECT, 1, head)
-        gather_round(DIRECT, 0, tail)
+        gather_round(DIRECT, 0, *tail)
         a_ref[mine, :] = pivot_rows[...]
         ready()
         gather_round(DIRECT, 2, head)
-        gather_round(DIRECT, 1, tail)
+        gather_round(DIRECT, 1, *tail)
         gather_round(RELAY, 0, late)
         if START:
             gather_round(RELAY, 1, early)
 
         def during(j):
             if j == 1:
-                gather_round(DIRECT, 2, tail)
+                gather_round(DIRECT, 2, *tail)
             if j in EARLY_AT:
                 gather_round(RELAY, START + 1 + EARLY_AT.index(j), early)
             if j in LATE_AT:
@@ -404,7 +404,7 @@
         tall = (size + 2 * height, size)
         shapes = [tall, tall, full, full, full, full, (2 * height, size), (size // NT, NT, NT)]
         shapes += [(NT, NT)] * 4 + [part] * 5 + [(3, *part), (2, *part)]
-        sems = [pltpu.SemaphoreType.DMA((2, 4, SLOTS))] * 2 + [pltpu.SemaphoreType.DMA((16,))] * 2
+        sems = [pltpu.SemaphoreType.DMA((2, 5, SLOTS))] * 2 + [pltpu.SemaphoreType.DMA((16,))] * 2
         blocks, solved = pl.pallas_call(
             kernel,
             out_shape=[jax.ShapeDtypeStruct((2, *part), F32)] * 2,

time: 115 us -> 115 us (level)
  no operation moved by 1% of the time
where the time goes in v7:
time: 115 us; the launch traced here: 114 us
  Pallas kernels  111 us (97%)
  local copies, waits for them, and re-layouts  2.46 us (2%)
    pallas_call x1, Pallas kernels, shards(): pl.pallas_call(kernel, out_shape=[jax.ShapeDtypeStruct((2, *part), F32)]...  111 us
    unnamed x4, local copies, waits for them, and re-layouts  2.46 us

profile of v7, /device:TPU:1, one launch (start us, length us, event | category | flops | bytes accessed | tf_op | source)
XLA Modules:
  0.0 114.2 jit_solution(7040427153475566337)
XLA Ops:
  0.6 111.1 %shard_map.50 = (f32[2,48,768]{2,1,0:T(8,128)}, f32[2,48,768]{2,1,0:T(8,128)}) custom-call(f32[2,48,768]{2,1,0:T(8,128)} %diag.1, f32[48,768]{1,0:T(8,128)} %bitcast.4, f32[48,768]{1,0:T(8,128)} %bitcast.5), custom_call_target="tpu_custom_call" | custom-call | tf_op jit(solution)/shard_map/pallas_call | solution.py:408
  111.8 0.0 copy-start
  111.8 1.7 %copy.7 = f32[2,48,768]{2,1,0:T(8,128)} copy(f32[2,48,768]{2,1,0:T(8,128)} %get-tuple-element.8) | data formatting | bytes 589824
  113.5 0.0 copy-done
  113.5 0.7 copy.8
Async XLA Ops:
  111.8 1.8 %copy-start = (f32[2,48,768]{2,1,0:T(8,128)S(1)}, f32[2,48,768]{2,1,0:T(8,128)}, u32[]{:S(2)}) copy-start(f32[2,48,768]{2,1,0:T(8,128)} %get-tuple-element.5) | copy-start | bytes 884740
